TPU v7x, 256 devices: a whole 4x4x8 slice. The times are simulated.
256 devices in a mesh: section: 4 (over z_hi), seq: 64 (over x, y, z_lo, core).
Axes of the slice: x: 4, y: 4, z: 8 (z_hi: 4, z_lo: 2; z = z_hi * 2 + z_lo), core: 2. Of those that a mesh axis runs over, the one named last changes fastest.
Arguments:
- memory: bfloat16 [8, 4096, 4096], P(None, 'seq', 'section'), may hold values from -6 to 6
- kv_weight: bfloat16 [4096, 4096], P('seq', 'section'), may hold values from -0.09375 to 0.09375
- mem_lengths: int32 [8], replicated, may hold values from 1024 to 4096, as said below
- queries: bfloat16 [16384, 2048], P('seq', 'section'), may hold values from -128 to 128
- out_weight: bfloat16 [2048, 4096], P('section'), may hold values from -0.125 to 0.125
- residual: bfloat16 [16384, 4096], P(('seq', 'section')), may hold values from -1.5 to 1.5
- norm_gain: float32 [4096], replicated, may hold values from 0.5 to 1.5
Outputs:
- hidden_out: bfloat16 [16384, 4096], P(('seq', 'section'))
- normed_out: bfloat16 [16384, 4096], P(('seq', 'section'))
Inputs may be any that keep to these rules, and one draw needn't show every extreme that they name: `mem_lengths`: valid memory positions of each proof state; positions at or beyond it are padding; at least one proof state has none.
All inputs are finite; a program needn't handle non-finite values.
Results may differ from a plain program's by a relative error of at most 0.012.
Values may be sent and summed in bfloat16 or wider, within the bound.
No kernel may reach another device: no remote copies, remote signals or barrier semaphores. Data moves between devices by JAX's collectives and lax.ppermute only.
A program may use at most 128 MiB of HBM per device.

v0:
```python
import functools
import math

import jax
import jax.numpy as jnp
from jax import lax
from jax.experimental import pallas as pl
from jax.experimental.pallas import tpu as pltpu
from jax.sharding import Mesh, PartitionSpec as P


DH = 256
VMEM_LIMIT = 16 << 20
BF = jnp.bfloat16
F32 = jnp.float32
X = "x"
Y = ("yh", "yl")
XY = ("x", "yh", "yl")
Z = "zh"
EXP_SCALE = math.log2(math.e) / math.sqrt(DH)
FWD = [(i, (i + 1) % 4) for i in range(4)]
BWD = [(i, (i + 3) % 4) for i in range(4)]


def swap(a, axis):
    return lax.ppermute(a, axis, [(0, 1), (1, 0)])


def beyond(a, axis):
    return [lax.ppermute(a, axis, [(i, (i + 4 - d) % 4) for i in range(4)]) for d in (1, 2, 3)]


def pair(a, b, index, axis=0):
    return jnp.where(index == 0, jnp.concatenate([a, b], axis), jnp.concatenate([b, a], axis))


def pick(a, b, index):
    return jnp.where(index == 0, a, b)


def kernel_call(kernel, outs, where, *args):
    spec = pl.BlockSpec(memory_space=pltpu.VMEM)
    args = [pltpu.with_memory_space_constraint(a, pltpu.VMEM) for a in args]
    return pl.pallas_call(
        kernel,
        out_shape=outs,
        in_specs=[pl.BlockSpec(memory_space=pltpu.SMEM)] + [spec] * len(args),
        out_specs=[spec] * len(outs),
        compiler_params=pltpu.CompilerParams(vmem_limit_bytes=VMEM_LIMIT),
    )(where, *args)


def project_kernel(where_ref, *refs):
    pieces, (w_mine, w_theirs, out_ref) = refs[:8], refs[8:]
    zh, x, y, c = where_ref[0], where_ref[1], where_ref[2], where_ref[3]
    acc = [jnp.zeros((512, 2 * DH), F32)] * 2
    near = [lax.rem(i + 4 - y, 4) for i in range(4)]
    for dz in range(4):
        dx = lax.rem(zh + dz + 4 - x, 4)
        rows = jnp.concatenate([pieces[2 * dz][...], pieces[2 * dz + 1][...]], 0)
        for j, w in enumerate((w_mine, w_theirs)):
            block = jnp.concatenate([w[dy, dx] for dy in near], 0)
            acc[j] = acc[j] + jnp.dot(rows, block, preferred_element_type=F32)
    out_ref[:, c] = acc[0].astype(BF).reshape(8, 64, 2 * DH)
    out_ref[:, 1 - c] = acc[1].astype(BF).reshape(8, 64, 2 * DH)


def project(where, pieces, weights):
    out = jax.ShapeDtypeStruct((8, 2, 64, 2 * DH), BF)
    return kernel_call(project_kernel, [out], where, *pieces, *weights)[0]


def attend_kernel(where_ref, q_ref, kv_ref, *outs):
    length, base = where_ref[0], where_ref[1]
    rows = kv_ref.shape[0]
    row = lax.broadcasted_iota(jnp.int32, (rows, 128), 0)
    position = (row >> 7) * 512 + base + (row & 127)
    bias = jnp.where(position < length, 0.0, -1e30)
    bias = jnp.concatenate([bias, bias], axis=1)
    keys = kv_ref[:, :DH]
    values = kv_ref[:, DH:].T
    for i in range(8):
        group = where_ref[2 + i // 2] * 2 + i % 2
        q = q_ref[pl.ds(pl.multiple_of(group * 256, 256), 256)]
        s = lax.dot_general(keys, q, (((1,), (1,)), ((), ())), preferred_element_type=F32) + bias
        high = jnp.max(s, axis=0, keepdims=True)
        p = jnp.exp2((s - high) * EXP_SCALE)
        total = jnp.sum(p, axis=0, keepdims=True)
        acc = jnp.dot(values, p.astype(BF), preferred_element_type=F32)
        lse = high * EXP_SCALE + jnp.log2(total)
        first = lse.astype(BF).astype(F32)
        second = (lse - first).astype(BF).astype(F32)
        stats = jnp.concatenate([first, second, lse - first - second, jnp.zeros((13, 256), F32)], 0)
        outs[i // 2][i % 2, :DH] = (acc * (1.0 / total)).astype(BF)
        outs[i // 2][i % 2, DH:] = stats.astype(BF)


def attend(where, q, kv):
    return kernel_call(attend_kernel, [jax.ShapeDtypeStruct((2, DH + 16, 256), BF)] * 4, where, q, kv)


def merge_kernel(where_ref, a_ref, b_ref, c_ref, d_ref, *outs):
    zh = where_ref[0]
    refs = (a_ref, b_ref, c_ref, d_ref)
    contexts = []
    for side in range(2):
        stats = [ref[side, DH:].astype(F32) for ref in refs]
        lse = [s[0:1] + s[1:2] + s[2:3] for s in stats]
        high = functools.reduce(jnp.maximum, lse)
        weight = [jnp.exp2(v - high) for v in lse]
        inverse = 1.0 / sum(weight)
        context = sum(ref[side, :DH].astype(F32) * (w * inverse) for ref, w in zip(refs, weight))
        contexts.append(context.T.astype(BF))
    for d in range(4):
        for m in range(4):

            @pl.when(lax.rem(zh + d, 4) == m)
            def _(d=d, m=m):
                for side in range(2):
                    outs[d][side * 64 : (side + 1) * 64] = contexts[side][m * 64 : (m + 1) * 64]


def merge(where, parts):
    return kernel_call(merge_kernel, [jax.ShapeDtypeStruct((128, DH), BF)] * 4, where, *parts)


def output_kernel(where_ref, *refs):
    c = where_ref[3]
    w_ref, out_mine, out_theirs = refs[4:]
    rows = jnp.concatenate([ref[...] for ref in refs[:4]], 1)
    for i in range(8):
        cols = slice(i * 512, (i + 1) * 512)
        acc = jnp.dot(rows, w_ref[:, cols], preferred_element_type=F32)
        low, high = acc[:64], acc[64:]
        out_mine[:, cols] = jnp.where(c == 0, low, high)
        out_theirs[:, cols] = jnp.where(c == 0, high, low)


def output(where, ctx, w):
    return kernel_call(output_kernel, [jax.ShapeDtypeStruct((64, 4096), F32)] * 2, where, *ctx, w)


def finish_kernel(where_ref, mine, other, residual, gain, hidden, normed):
    x = residual[...].astype(F32) + (mine[...] + other[...])
    scale = lax.rsqrt(jnp.mean(x * x, -1, keepdims=True) + 1e-06)
    hidden[...] = x.astype(BF)
    normed[...] = (x * scale * gain[...]).astype(BF)


def finish(where, *args):
    return kernel_call(finish_kernel, [jax.ShapeDtypeStruct(args[2].shape, BF)] * 2, where, *args)


def shards(memory, kv_weight, mem_lengths, queries, out_weight, residual, norm_gain):
    zh, x, yh, yl, zl, c = (lax.axis_index(a) for a in (Z, X, "yh", "yl", "zl", "c"))
    y = yh * 2 + yl
    where = jnp.stack([zh, x, y, c]).astype(jnp.int32)

    mine = pick(kv_weight[:, :512], kv_weight[:, 512:], c)
    theirs = pick(kv_weight[:, 512:], kv_weight[:, :512], c)
    w_c = swap(theirs, "c")
    w_z = swap(mine, "zl")
    w_zc = lax.ppermute(theirs, ("zl", "c"), [(i, 3 - i) for i in range(4)])
    rows = pair(pair(mine, w_c, c), pair(w_z, w_zc, c), zl)
    w_near = beyond(rows, X)
    w_near = jnp.stack([rows, *w_near])
    w_prev = lax.ppermute(w_near, Y, FWD)
    w_next = lax.ppermute(w_near, Y, BWD)
    w_far_a = lax.ppermute(w_prev[:2], Y, FWD)
    w_far_b = lax.ppermute(w_next[2:], Y, BWD)
    w_mine = jnp.concatenate([w_near, w_next, w_far_a, w_far_b, w_prev], 0).reshape((4,) + w_near.shape)
    w_theirs = swap(w_mine, "c")

    mem_a, mem_b = memory[:4].reshape(256, 1024), memory[4:].reshape(256, 1024)
    prev_a = lax.ppermute(mem_a, Z, FWD)
    next_a = lax.ppermute(mem_a, Z, BWD)
    next_b = lax.ppermute(mem_b, Z, BWD)
    prev_b = lax.ppermute(mem_b, Z, FWD)
    far_a = lax.ppermute(prev_a, Z, FWD)
    far_b = lax.ppermute(next_b, Z, BWD)
    pieces = (mem_a, mem_b, next_a, next_b, far_a, far_b, prev_a, prev_b)

    ow = lax.dynamic_slice(out_weight, (c * DH, (x * 4 + y) * 256), (DH, 256))
    ow = [ow, *beyond(ow, Z)]
    ow = jnp.concatenate(ow, 0)

    ow = lax.all_gather(ow, XY, axis=1, tiled=True)

    other = pick(queries[:, DH:], queries[:, :DH], c)
    other = swap(other, "c")
    q = pair(pick(queries[:, :DH], queries[:, DH:], c), other, c)
    other = swap(q, "zl")
    q = pair(q, other, zl)
    other = swap(q, "yl")
    q = pair(q, other, yl)

    length = lax.dynamic_index_in_dim(mem_lengths, x * 2 + yh, 0, keepdims=False)
    here = yl * 2 + zl
    here = jnp.stack([length, yl * 256 + zl * 128, here, here ^ 1, here ^ 2, here ^ 3]).astype(jnp.int32)
    both = project(where, pieces, (w_mine, w_theirs))
    both = lax.all_to_all(both.reshape(16, 64, 512), (X, "yh", "c"), 0, 0, tiled=True)
    own, to_zl, to_yl, to_both = attend(here, q, both.reshape(1024, 512))

    parts = (
        own,
        swap(to_zl, "zl"),
        swap(to_yl, "yl"),
        lax.ppermute(to_both, ("yl", "zl"), [(i, 3 - i) for i in range(4)]),
    )
    pieces = merge(where, parts)
    ctx = [pieces[0]] + [lax.ppermute(pieces[4 - d], Z, [(i, (i + 4 - d) % 4) for i in range(4)]) for d in (1, 2, 3)]
    mine, theirs = output(where, ctx, ow)
    return tuple(finish(where, mine, swap(theirs, "c"), residual, norm_gain.reshape(1, -1)))


def solution(mesh):
    fine = Mesh(mesh.devices.reshape(4, 4, 2, 2, 2, 2), (Z, X, "yh", "yl", "zl", "c"))
    seq = (X, "yh", "yl", "zl", "c")
    in_specs = (
        P(None, seq, Z),
        P(seq, Z),
        P(),
        P(seq, Z),
        P(Z, None),
        P(seq + (Z,), None),
        P(),
    )
    out_specs = (P(seq + (Z,), None), P(seq + (Z,), None))
    return jax.shard_map(shards, mesh=fine, in_specs=in_specs, out_specs=out_specs, check_vma=False)
```

profile of v0, /device:TPU:1, one launch (start us, length us, event | category | flops | bytes accessed | tf_op | source)
XLA Modules:
  0.0 283.3 jit_solution(4288103693864350438)
XLA Ops:
  8.2 6.9 %collective-permute-start.26 = (bf16[256,256]{1,0:T(8,128)(2,1)S(1)}, bf16[256,256]{1,0:T(8,128)(2,1)S(1)}, u32[]{:S(2)}, u32[]{:S(2)}) collective-permute-start(bf16[256,256]{1,0:T(8,128)(2,1)S(1)} %dynamic_slice.8), channel_id=1, source_target_pairs={{0,192},{64,0},{128,64},{192,128},{1,193},{65,1},{129,65},{193,129... | collective-permute-start | bytes 393224 | tf_op jit(solution)/shard_map/ppermute | solution.py:30
  15.1 1.0 collective-permute-start.27
  16.1 2.3 collective-permute-start.28
  18.3 7.9 %collective-permute-done.27 = bf16[256,256]{1,0:T(8,128)(2,1)S(1)} collective-permute-done((bf16[256,256]{1,0:T(8,128)(2,1)S(1)}, bf16[256,256]{1,0:T(8,128)(2,1)S(1)}, u32[]{:S(2)}, u32[]{:S(2)}) %collective-permute-start.27) | collective-permute-done | bytes 131104 | tf_op jit(solution)/shard_map/ppermute | solution.py:30
  28.1 2.8 collective-permute-start.9
  30.9 1.6 collective-permute-start.11
  32.5 3.1 %collective-permute-done.10 = bf16[64,512]{1,0:T(8,128)(2,1)S(1)} collective-permute-done((bf16[64,512]{1,0:T(8,128)(2,1)S(1)}, bf16[64,512]{1,0:T(8,128)(2,1)S(1)}, u32[]{:S(2)}, u32[]{:S(2)}) %collective-permute-start.10) | collective-permute-done | bytes 65568 | tf_op jit(solution)/shard_map/ppermute | solution.py:26
  35.6 2.6 collective-permute-start.12
  40.1 3.0 %collective-permute-done.12 = bf16[256,512]{1,0:T(8,128)(2,1)S(1)} collective-permute-done((bf16[256,512]{1,0:T(8,128)(2,1)S(1)}, bf16[256,512]{1,0:T(8,128)(2,1)S(1)}, u32[]{:S(2)}, u32[]{:S(2)}) %collective-permute-start.12) | collective-permute-done | bytes 262176 | tf_op jit(solution)/shard_map/ppermute | solution.py:30
  43.1 2.7 collective-permute-done.13
  45.8 11.5 %collective-permute-done.14 = bf16[256,512]{1,0:T(8,128)(2,1)S(1)} collective-permute-done((bf16[256,512]{1,0:T(8,128)(2,1)S(1)}, bf16[256,512]{1,0:T(8,128)(2,1)S(1)}, u32[]{:S(2)}, u32[]{:S(2)}) %collective-permute-start.14) | collective-permute-done | bytes 262176 | tf_op jit(solution)/shard_map/ppermute | solution.py:30
  57.5 1.5 collective-permute-start.16
  58.9 1.7 collective-permute-start.15
  61.4 26.1 %collective-permute-done.16 = bf16[4,256,512]{2,1,0:T(8,128)(2,1)S(1)} collective-permute-done((bf16[4,256,512]{2,1,0:T(8,128)(2,1)S(1)}, bf16[4,256,512]{2,1,0:T(8,128)(2,1)S(1)}, u32[]{:S(2)}, u32[]{:S(2)}) %collective-permute-start.16) | collective-permute-done | bytes 1048608 | tf_op jit(solution)/shard_map/ppermute | solution.py:167
  87.7 1.4 collective-permute-done.15
  89.2 3.6 %collective-permute-start.18 = (bf16[2,256,512]{2,1,0:T(8,128)(2,1)S(1)}, bf16[2,256,512]{2,1,0:T(8,128)(2,1)S(1)}, u32[]{:S(2)}, u32[]{:S(2)}) collective-permute-start(bf16[2,256,512]{2,1,0:T(8,128)(2,1)S(1)} %slice.37), channel_id=1, source_target_pairs={{0,12},{4,0},{8,4},{12,8},{1,13},{5,1},{9,5},{13,9},{2,14},{6,2},{... | collective-permute-start | bytes 1572872 | tf_op jit(solution)/shard_map/ppermute | solution.py:170
  94.2 1.0 constant_dynamic-update-slice_fusion.3
  95.3 14.6 %collective-permute-done.17 = bf16[2,256,512]{2,1,0:T(8,128)(2,1)S(1)} collective-permute-done((bf16[2,256,512]{2,1,0:T(8,128)(2,1)S(1)}, bf16[2,256,512]{2,1,0:T(8,128)(2,1)S(1)}, u32[]{:S(2)}, u32[]{:S(2)}) %collective-permute-start.17) | collective-permute-done | bytes 524320 | tf_op jit(solution)/shard_map/ppermute | solution.py:169
  111.8 1.0 constant_dynamic-update-slice_fusion
  112.8 3.3 %collective-permute-start.19 = (bf16[4,4,256,512]{3,2,1,0:T(8,128)(2,1)}, bf16[4,4,256,512]{3,2,1,0:T(8,128)(2,1)}, u32[]{:S(2)}, u32[]{:S(2)}) collective-permute-start(bf16[4,4,256,512]{3,2,1,0:T(8,128)(2,1)} %bitcast.16.refs_8_), channel_id=1, source_target_pairs={{0,1},{1,0},{2,3},{3,2},{4,5},{5,4},{6,7},{7,6},{8,9},{9,8},{10,11... | collective-permute-start | bytes 12582920 | tf_op jit(solution)/shard_map/ppermute | solution.py:26
  116.2 1.2 collective-permute-start.5
  117.4 2.5 collective-permute-start.4
  120.0 2.5 collective-permute-start.3
  123.2 1.0 collective-permute-done
  124.5 7.6 %collective-permute-done.5.refs_6_ = bf16[256,1024]{1,0:T(8,128)(2,1)S(1)} collective-permute-done((bf16[256,1024]{1,0:T(8,128)(2,1)S(1)}, bf16[256,1024]{1,0:T(8,128)(2,1)S(1)}, u32[]{:S(2)}, u32[]{:S(2)}) %collective-permute-start.5) | collective-permute-done | bytes 524320 | tf_op jit(solution)/shard_map/ppermute | solution.py:175
  132.1 1.7 collective-permute-start.6
  134.7 1.1 collective-permute-start.7
  135.8 10.2 %collective-permute-done.3.refs_2_ = bf16[256,1024]{1,0:T(8,128)(2,1)S(1)} collective-permute-done((bf16[256,1024]{1,0:T(8,128)(2,1)S(1)}, bf16[256,1024]{1,0:T(8,128)(2,1)S(1)}, u32[]{:S(2)}, u32[]{:S(2)}) %collective-permute-start.3) | collective-permute-done | bytes 524320 | tf_op jit(solution)/shard_map/ppermute | solution.py:176
  146.0 36.1 %collective-permute-start.1 = (bf16[512,256]{1,0:T(8,128)(2,1)S(1)}, bf16[512,256]{1,0:T(8,128)(2,1)}, u32[]{:S(2)}, u32[]{:S(2)}) collective-permute-start(bf16[512,256]{1,0:T(8,128)(2,1)S(1)} %maximum_select_fusion.2), channel_id=1, source_target_pairs={{0,2},{2,0},{1,3},{3,1},{4,6},{6,4},{5,7},{7,5},{8,10},{10,8},{9,1... | collective-permute-start | bytes 786440 | tf_op jit(solution)/shard_map/ppermute | solution.py:26
  182.2 9.3 %shard_map.86 = bf16[8,2,64,512]{3,2,1,0:T(8,128)(2,1)} custom-call(s32[4]{0:T(128)S(1)} %pad_add_fusion.where_ref, bf16[256,1024]{1,0:T(8,128)(2,1)S(1)} %bitcast.29, bf16[256,1024]{1,0:T(8,128)(2,1)S(1)} %bitcast.26, bf16[256,1024]{1,0:T(8,128)(2,1)S(1)} %collective-permute-done.3.refs_2_, bf16[256,1024]{1,0:T(8,128)(2,1)S(1)} %collective-permute-done.4.refs_3_, ...), custom_call_target="tpu_custom_call" | custom-call | tf_op jit(solution)/shard_map/pallas_call | solution.py:44
  191.5 10.7 %all-to-all-start = ((bf16[16,64,512]{2,1,0:T(8,128)(2,1)}), bf16[16,64,512]{2,1,0:T(8,128)(2,1)S(1)}, u32[]{:S(2)}, u32[]{:S(2)}) async-start(bf16[16,64,512]{2,1,0:T(8,128)(2,1)} %bitcast.17), calls=%async_computation | async-start | bytes 2097152 | tf_op jit(solution)/shard_map/all_to_all | solution.py:201
  202.2 1.2 maximum_select_fusion.1
  204.9 20.3 %collective-permute-done.2 = bf16[1024,256]{1,0:T(8,128)(2,1)} collective-permute-done((bf16[1024,256]{1,0:T(8,128)(2,1)S(1)}, bf16[1024,256]{1,0:T(8,128)(2,1)}, u32[]{:S(2)}, u32[]{:S(2)}) %collective-permute-start.2) | collective-permute-done | bytes 524320 | tf_op jit(solution)/shard_map/ppermute | solution.py:26
  225.2 1.5 maximum_select_fusion.q_ref
  226.7 4.7 %shard_map.87 = (bf16[2,272,256]{2,1,0:T(8,128)(2,1)S(1)}, bf16[2,272,256]{2,1,0:T(8,128)(2,1)S(1)}, bf16[2,272,256]{2,1,0:T(8,128)(2,1)S(1)}, bf16[2,272,256]{2,1,0:T(8,128)(2,1)S(1)}) custom-call(s32[6]{0:T(128)S(1)} %stack.57.where_ref, bf16[2048,256]{1,0:T(8,128)(2,1)S(1)} %maximum_select_fusion.q_ref, bf16[1024,512]{1,0:T(8,128)(2,1)S(1)} %bitcast.23), custom_call_target="tpu_custom_call" | custom-call | tf_op jit(solution)/shard_map/pallas_call | solution.py:44
  231.4 6.7 %collective-permute-start.20 = (bf16[2,272,256]{2,1,0:T(8,128)(2,1)S(1)}, bf16[2,272,256]{2,1,0:T(8,128)(2,1)S(1)}, u32[]{:S(2)}, u32[]{:S(2)}) collective-permute-start(bf16[2,272,256]{2,1,0:T(8,128)(2,1)S(1)} %get-tuple-element.13), channel_id=1, source_target_pairs={{0,2},{2,0},{1,3},{3,1},{4,6},{6,4},{5,7},{7,5},{8,10},{10,8},{9,1... | collective-permute-start | bytes 835592 | tf_op jit(solution)/shard_map/ppermute | solution.py:26
  239.6 4.9 %collective-permute-done.20.b_ref = bf16[2,272,256]{2,1,0:T(8,128)(2,1)S(1)} collective-permute-done((bf16[2,272,256]{2,1,0:T(8,128)(2,1)S(1)}, bf16[2,272,256]{2,1,0:T(8,128)(2,1)S(1)}, u32[]{:S(2)}, u32[]{:S(2)}) %collective-permute-start.20) | collective-permute-done | bytes 278560 | tf_op jit(solution)/shard_map/ppermute | solution.py:26
  244.5 1.5 collective-permute-done.21.c_ref
  246.0 4.8 %collective-permute-done.22.d_ref = bf16[2,272,256]{2,1,0:T(8,128)(2,1)S(1)} collective-permute-done((bf16[2,272,256]{2,1,0:T(8,128)(2,1)S(1)}, bf16[2,272,256]{2,1,0:T(8,128)(2,1)S(1)}, u32[]{:S(2)}, u32[]{:S(2)}) %collective-permute-start.22) | collective-permute-done | bytes 278560 | tf_op jit(solution)/shard_map/ppermute | solution.py:208
  251.8 2.2 collective-permute-start.23
  254.0 4.5 %collective-permute-start.24 = (bf16[128,256]{1,0:T(8,128)(2,1)S(1)}, bf16[128,256]{1,0:T(8,128)(2,1)S(1)}, u32[]{:S(2)}, u32[]{:S(2)}) collective-permute-start(bf16[128,256]{1,0:T(8,128)(2,1)S(1)} %get-tuple-element.18), channel_id=1, source_target_pairs={{0,128},{64,192},{128,0},{192,64},{1,129},{65,193},{129,1},{193,65... | collective-permute-start | bytes 196616 | tf_op jit(solution)/shard_map/ppermute | solution.py:211
  258.5 2.5 collective-permute-done.24.refs_2_
  261.0 3.2 %collective-permute-done.25.refs_3_ = bf16[128,256]{1,0:T(8,128)(2,1)S(1)} collective-permute-done((bf16[128,256]{1,0:T(8,128)(2,1)S(1)}, bf16[128,256]{1,0:T(8,128)(2,1)S(1)}, u32[]{:S(2)}, u32[]{:S(2)}) %collective-permute-start.25) | collective-permute-done | bytes 65568 | tf_op jit(solution)/shard_map/ppermute | solution.py:211
  264.2 3.4 %copy-done = bf16[1024,4096]{1,0:T(8,128)(2,1)S(1)} copy-done((bf16[1024,4096]{1,0:T(8,128)(2,1)S(1)}, bf16[1024,4096]{1,0:T(8,128)(2,1)}, u32[]{:S(2)}) %copy-start) | copy-done | bytes 8388632
  267.6 1.9 shard_map.89
  269.5 3.0 %collective-permute-start.29 = (f32[64,4096]{1,0:T(8,128)S(1)}, f32[64,4096]{1,0:T(8,128)S(1)}, u32[]{:S(2)}, u32[]{:S(2)}) collective-permute-start(f32[64,4096]{1,0:T(8,128)S(1)} %get-tuple-element.21), channel_id=1, source_target_pairs={{0,1},{1,0},{2,3},{3,2},{4,5},{5,4},{6,7},{7,6},{8,9},{9,8},{10,11... | collective-permute-start | bytes 3145736 | tf_op jit(solution)/shard_map/ppermute | solution.py:26
  272.5 2.3 collective-permute-done.29.other
  274.7 1.7 shard_map.90
  (59 shorter events, 15.3 us)
Async XLA Ops:
  7.2 257.1 %all-gather.2.cloned.1.call-start = ((), (), s32[]{:S(2)}) async-start(), calls=%async_computation.1 | async-start | bytes 8912896 | tf_op jit(solution)/shard_map/all_gather | solution.py:187
  8.2 10.2 %collective-permute-start.26 = (bf16[256,256]{1,0:T(8,128)(2,1)S(1)}, bf16[256,256]{1,0:T(8,128)(2,1)S(1)}, u32[]{:S(2)}, u32[]{:S(2)}) collective-permute-start(bf16[256,256]{1,0:T(8,128)(2,1)S(1)} %dynamic_slice.8), channel_id=1, source_target_pairs={{0,192},{64,0},{128,64},{192,128},{1,193},{65,1},{129,65},{193,129... | collective-permute-start | bytes 393224 | tf_op jit(solution)/shard_map/ppermute | solution.py:30
  15.1 11.1 %collective-permute-start.27 = (bf16[256,256]{1,0:T(8,128)(2,1)S(1)}, bf16[256,256]{1,0:T(8,128)(2,1)S(1)}, u32[]{:S(2)}, u32[]{:S(2)}) collective-permute-start(bf16[256,256]{1,0:T(8,128)(2,1)S(1)} %dynamic_slice.8), channel_id=1, source_target_pairs={{0,128},{64,192},{128,0},{192,64},{1,129},{65,193},{129,1},{193,65... | collective-permute-start | bytes 393224 | tf_op jit(solution)/shard_map/ppermute | solution.py:30
  16.1 10.2 %collective-permute-start.28 = (bf16[256,256]{1,0:T(8,128)(2,1)S(1)}, bf16[256,256]{1,0:T(8,128)(2,1)S(1)}, u32[]{:S(2)}, u32[]{:S(2)}) collective-permute-start(bf16[256,256]{1,0:T(8,128)(2,1)S(1)} %dynamic_slice.8), channel_id=1, source_target_pairs={{0,64},{64,128},{128,192},{192,0},{1,65},{65,129},{129,193},{193,1... | collective-permute-start | bytes 393224 | tf_op jit(solution)/shard_map/ppermute | solution.py:30
  28.1 4.4 %collective-permute-start.9 = (bf16[64,512]{1,0:T(8,128)(2,1)S(1)}, bf16[64,512]{1,0:T(8,128)(2,1)S(1)}, u32[]{:S(2)}, u32[]{:S(2)}) collective-permute-start(bf16[64,512]{1,0:T(8,128)(2,1)S(1)} %get-tuple-element.29), channel_id=1, source_target_pairs={{0,1},{1,0},{2,3},{3,2},{4,5},{5,4},{6,7},{7,6},{8,9},{9,8},{10,11... | collective-permute-start | bytes 196616 | tf_op jit(solution)/shard_map/ppermute | solution.py:26
  30.9 4.7 %collective-permute-start.11 = (bf16[64,512]{1,0:T(8,128)(2,1)S(1)}, bf16[64,512]{1,0:T(8,128)(2,1)S(1)}, u32[]{:S(2)}, u32[]{:S(2)}) collective-permute-start(bf16[64,512]{1,0:T(8,128)(2,1)S(1)} %get-tuple-element.29), channel_id=1, source_target_pairs={{0,3},{1,2},{2,1},{3,0},{4,7},{5,6},{6,5},{7,4},{8,11},{9,10},{10,... | collective-permute-start | bytes 196616 | tf_op jit(solution)/shard_map/ppermute | solution.py:163
  32.4 3.1 %collective-permute-start.10 = (bf16[64,512]{1,0:T(8,128)(2,1)S(1)}, bf16[64,512]{1,0:T(8,128)(2,1)S(1)}, u32[]{:S(2)}, u32[]{:S(2)}) collective-permute-start(bf16[64,512]{1,0:T(8,128)(2,1)S(1)} %get-tuple-element.28), channel_id=1, source_target_pairs={{0,2},{2,0},{1,3},{3,1},{4,6},{6,4},{5,7},{7,5},{8,10},{10,8},{9,1... | collective-permute-start | bytes 196616 | tf_op jit(solution)/shard_map/ppermute | solution.py:26
  35.6 7.5 %collective-permute-start.12 = (bf16[256,512]{1,0:T(8,128)(2,1)S(1)}, bf16[256,512]{1,0:T(8,128)(2,1)S(1)}, u32[]{:S(2)}, u32[]{:S(2)}) collective-permute-start(bf16[256,512]{1,0:T(8,128)(2,1)S(1)} %maximum_select_fusion.4), channel_id=1, source_target_pairs={{0,48},{16,0},{32,16},{48,32},{1,49},{17,1},{33,17},{49,33},{2,50}... | collective-permute-start | bytes 786440 | tf_op jit(solution)/shard_map/ppermute | solution.py:30
  38.2 7.6 %collective-permute-start.13 = (bf16[256,512]{1,0:T(8,128)(2,1)S(1)}, bf16[256,512]{1,0:T(8,128)(2,1)S(1)}, u32[]{:S(2)}, u32[]{:S(2)}) collective-permute-start(bf16[256,512]{1,0:T(8,128)(2,1)S(1)} %maximum_select_fusion.4), channel_id=1, source_target_pairs={{0,32},{16,48},{32,0},{48,16},{1,33},{17,49},{33,1},{49,17},{2,34}... | collective-permute-start | bytes 786440 | tf_op jit(solution)/shard_map/ppermute | solution.py:30
  38.7 18.6 %collective-permute-start.14 = (bf16[256,512]{1,0:T(8,128)(2,1)S(1)}, bf16[256,512]{1,0:T(8,128)(2,1)S(1)}, u32[]{:S(2)}, u32[]{:S(2)}) collective-permute-start(bf16[256,512]{1,0:T(8,128)(2,1)S(1)} %maximum_select_fusion.4), channel_id=1, source_target_pairs={{0,16},{16,32},{32,48},{48,0},{1,17},{17,33},{33,49},{49,1},{2,18}... | collective-permute-start | bytes 786440 | tf_op jit(solution)/shard_map/ppermute | solution.py:30
  57.5 30.0 %collective-permute-start.16 = (bf16[4,256,512]{2,1,0:T(8,128)(2,1)S(1)}, bf16[4,256,512]{2,1,0:T(8,128)(2,1)S(1)}, u32[]{:S(2)}, u32[]{:S(2)}) collective-permute-start(bf16[4,256,512]{2,1,0:T(8,128)(2,1)S(1)} %pad_maximum_fusion), channel_id=1, source_target_pairs={{0,4},{4,8},{8,12},{12,0},{1,5},{5,9},{9,13},{13,1},{2,6},{6,10},{... | collective-permute-start | bytes 3145736 | tf_op jit(solution)/shard_map/ppermute | solution.py:167
  58.9 30.3 %collective-permute-start.15 = (bf16[4,256,512]{2,1,0:T(8,128)(2,1)S(1)}, bf16[4,256,512]{2,1,0:T(8,128)(2,1)S(1)}, u32[]{:S(2)}, u32[]{:S(2)}) collective-permute-start(bf16[4,256,512]{2,1,0:T(8,128)(2,1)S(1)} %pad_maximum_fusion), channel_id=1, source_target_pairs={{0,12},{4,0},{8,4},{12,8},{1,13},{5,1},{9,5},{13,9},{2,14},{6,2},{... | collective-permute-start | bytes 3145736 | tf_op jit(solution)/shard_map/ppermute | solution.py:168
  87.5 28.7 %copy-start.3 = (bf16[8,64,1024]{2,1,0:T(8,128)(2,1)S(1)}, bf16[8,64,1024]{2,1,0:T(8,128)(2,1)}, u32[]{:S(2)}) copy-start(bf16[8,64,1024]{2,1,0:T(8,128)(2,1)} %param.7) | copy-start | bytes 3145732
  87.5 22.4 %collective-permute-start.17 = (bf16[2,256,512]{2,1,0:T(8,128)(2,1)S(1)}, bf16[2,256,512]{2,1,0:T(8,128)(2,1)S(1)}, u32[]{:S(2)}, u32[]{:S(2)}) collective-permute-start(bf16[2,256,512]{2,1,0:T(8,128)(2,1)S(1)} %slice.36), channel_id=1, source_target_pairs={{0,4},{4,8},{8,12},{12,0},{1,5},{5,9},{9,13},{13,1},{2,6},{6,10},{... | collective-permute-start | bytes 1572872 | tf_op jit(solution)/shard_map/ppermute | solution.py:169
  89.2 21.7 %collective-permute-start.18 = (bf16[2,256,512]{2,1,0:T(8,128)(2,1)S(1)}, bf16[2,256,512]{2,1,0:T(8,128)(2,1)S(1)}, u32[]{:S(2)}, u32[]{:S(2)}) collective-permute-start(bf16[2,256,512]{2,1,0:T(8,128)(2,1)S(1)} %slice.37), channel_id=1, source_target_pairs={{0,12},{4,0},{8,4},{12,8},{1,13},{5,1},{9,5},{13,9},{2,14},{6,2},{... | collective-permute-start | bytes 1572872 | tf_op jit(solution)/shard_map/ppermute | solution.py:170
  94.2 28.2 %copy-start.4 = (bf16[256,512]{1,0:T(8,128)(2,1)S(1)}, bf16[256,512]{1,0:T(8,128)(2,1)}, u32[]{:S(2)}) copy-start(bf16[256,512]{1,0:T(8,128)(2,1)} %param.10) | copy-start | bytes 786436
  112.8 69.4 %collective-permute-start.19 = (bf16[4,4,256,512]{3,2,1,0:T(8,128)(2,1)}, bf16[4,4,256,512]{3,2,1,0:T(8,128)(2,1)}, u32[]{:S(2)}, u32[]{:S(2)}) collective-permute-start(bf16[4,4,256,512]{3,2,1,0:T(8,128)(2,1)} %bitcast.16.refs_8_), channel_id=1, source_target_pairs={{0,1},{1,0},{2,3},{3,2},{4,5},{5,4},{6,7},{7,6},{8,9},{9,8},{10,11... | collective-permute-start | bytes 12582920 | tf_op jit(solution)/shard_map/ppermute | solution.py:26
  116.2 15.9 %collective-permute-start.5 = (bf16[256,1024]{1,0:T(8,128)(2,1)S(1)}, bf16[256,1024]{1,0:T(8,128)(2,1)S(1)}, u32[]{:S(2)}, u32[]{:S(2)}) collective-permute-start(bf16[256,1024]{1,0:T(8,128)(2,1)S(1)} %bitcast.27), channel_id=1, source_target_pairs={{0,64},{64,128},{128,192},{192,0},{1,65},{65,129},{129,193},{193,1... | collective-permute-start | bytes 1572872 | tf_op jit(solution)/shard_map/ppermute | solution.py:175
  117.4 17.2 %collective-permute-start.4 = (bf16[256,1024]{1,0:T(8,128)(2,1)S(1)}, bf16[256,1024]{1,0:T(8,128)(2,1)S(1)}, u32[]{:S(2)}, u32[]{:S(2)}) collective-permute-start(bf16[256,1024]{1,0:T(8,128)(2,1)S(1)} %bitcast.24), channel_id=1, source_target_pairs={{0,192},{64,0},{128,64},{192,128},{1,193},{65,1},{129,65},{193,129... | collective-permute-start | bytes 1572872 | tf_op jit(solution)/shard_map/ppermute | solution.py:177
  120.0 26.0 %collective-permute-start.3 = (bf16[256,1024]{1,0:T(8,128)(2,1)S(1)}, bf16[256,1024]{1,0:T(8,128)(2,1)S(1)}, u32[]{:S(2)}, u32[]{:S(2)}) collective-permute-start(bf16[256,1024]{1,0:T(8,128)(2,1)S(1)} %bitcast.28), channel_id=1, source_target_pairs={{0,192},{64,0},{128,64},{192,128},{1,193},{65,1},{129,65},{193,129... | collective-permute-start | bytes 1572872 | tf_op jit(solution)/shard_map/ppermute | solution.py:176
  122.5 1.7 collective-permute-start
  124.2 58.0 %collective-permute-start.8 = (bf16[256,1024]{1,0:T(8,128)(2,1)S(1)}, bf16[256,1024]{1,0:T(8,128)(2,1)S(1)}, u32[]{:S(2)}, u32[]{:S(2)}) collective-permute-start(bf16[256,1024]{1,0:T(8,128)(2,1)S(1)} %bitcast.25), channel_id=1, source_target_pairs={{0,64},{64,128},{128,192},{192,0},{1,65},{65,129},{129,193},{193,1... | collective-permute-start | bytes 1572872 | tf_op jit(solution)/shard_map/ppermute | solution.py:178
  132.1 50.1 %collective-permute-start.6 = (bf16[256,1024]{1,0:T(8,128)(2,1)S(1)}, bf16[256,1024]{1,0:T(8,128)(2,1)}, u32[]{:S(2)}, u32[]{:S(2)}) collective-permute-start(bf16[256,1024]{1,0:T(8,128)(2,1)S(1)} %collective-permute-done.5.refs_6_), channel_id=1, source_target_pairs={{0,64},{64,128},{128,192},{192,0},{1,65},{65,129},{129,193},{193,1... | collective-permute-start | bytes 1572872 | tf_op jit(solution)/shard_map/ppermute | solution.py:179
  134.7 47.5 %collective-permute-start.7 = (bf16[256,1024]{1,0:T(8,128)(2,1)S(1)}, bf16[256,1024]{1,0:T(8,128)(2,1)}, u32[]{:S(2)}, u32[]{:S(2)}) collective-permute-start(bf16[256,1024]{1,0:T(8,128)(2,1)S(1)} %collective-permute-done.4.refs_3_), channel_id=1, source_target_pairs={{0,192},{64,0},{128,64},{192,128},{1,193},{65,1},{129,65},{193,129... | collective-permute-start | bytes 1572872 | tf_op jit(solution)/shard_map/ppermute | solution.py:180
  146.0 56.2 %collective-permute-start.1 = (bf16[512,256]{1,0:T(8,128)(2,1)S(1)}, bf16[512,256]{1,0:T(8,128)(2,1)}, u32[]{:S(2)}, u32[]{:S(2)}) collective-permute-start(bf16[512,256]{1,0:T(8,128)(2,1)S(1)} %maximum_select_fusion.2), channel_id=1, source_target_pairs={{0,2},{2,0},{1,3},{3,1},{4,6},{6,4},{5,7},{7,5},{8,10},{10,8},{9,1... | collective-permute-start | bytes 786440 | tf_op jit(solution)/shard_map/ppermute | solution.py:26
  182.2 21.4 %copy-start.5 = (s32[8]{0:T(128)S(1)}, s32[8]{0:T(128)}, u32[]{:S(2)}) copy-start(s32[8]{0:T(128)} %param.9) | copy-start | bytes 100
  191.5 35.2 %all-to-all-start = ((bf16[16,64,512]{2,1,0:T(8,128)(2,1)}), bf16[16,64,512]{2,1,0:T(8,128)(2,1)S(1)}, u32[]{:S(2)}, u32[]{:S(2)}) async-start(bf16[16,64,512]{2,1,0:T(8,128)(2,1)} %bitcast.17), calls=%async_computation | async-start | bytes 2097152 | tf_op jit(solution)/shard_map/all_to_all | solution.py:201
  203.5 21.7 %collective-permute-start.2 = (bf16[1024,256]{1,0:T(8,128)(2,1)S(1)}, bf16[1024,256]{1,0:T(8,128)(2,1)}, u32[]{:S(2)}, u32[]{:S(2)}) collective-permute-start(bf16[1024,256]{1,0:T(8,128)(2,1)S(1)} %maximum_select_fusion.1), channel_id=1, source_target_pairs={{0,4},{4,0},{1,5},{5,1},{2,6},{6,2},{3,7},{7,3},{8,12},{12,8},{9,1... | collective-permute-start | bytes 1572872 | tf_op jit(solution)/shard_map/ppermute | solution.py:26
  231.4 13.1 %collective-permute-start.20 = (bf16[2,272,256]{2,1,0:T(8,128)(2,1)S(1)}, bf16[2,272,256]{2,1,0:T(8,128)(2,1)S(1)}, u32[]{:S(2)}, u32[]{:S(2)}) collective-permute-start(bf16[2,272,256]{2,1,0:T(8,128)(2,1)S(1)} %get-tuple-element.13), channel_id=1, source_target_pairs={{0,2},{2,0},{1,3},{3,1},{4,6},{6,4},{5,7},{7,5},{8,10},{10,8},{9,1... | collective-permute-start | bytes 835592 | tf_op jit(solution)/shard_map/ppermute | solution.py:26
  238.1 7.9 %collective-permute-start.21 = (bf16[2,272,256]{2,1,0:T(8,128)(2,1)S(1)}, bf16[2,272,256]{2,1,0:T(8,128)(2,1)S(1)}, u32[]{:S(2)}, u32[]{:S(2)}) collective-permute-start(bf16[2,272,256]{2,1,0:T(8,128)(2,1)S(1)} %get-tuple-element.14), channel_id=1, source_target_pairs={{0,4},{4,0},{1,5},{5,1},{2,6},{6,2},{3,7},{7,3},{8,12},{12,8},{9,1... | collective-permute-start | bytes 835592 | tf_op jit(solution)/shard_map/ppermute | solution.py:26
  238.7 12.1 %collective-permute-start.22 = (bf16[2,272,256]{2,1,0:T(8,128)(2,1)S(1)}, bf16[2,272,256]{2,1,0:T(8,128)(2,1)S(1)}, u32[]{:S(2)}, u32[]{:S(2)}) collective-permute-start(bf16[2,272,256]{2,1,0:T(8,128)(2,1)S(1)} %get-tuple-element.15), channel_id=1, source_target_pairs={{0,6},{2,4},{4,2},{6,0},{1,7},{3,5},{5,3},{7,1},{8,14},{10,12},{12... | collective-permute-start | bytes 835592 | tf_op jit(solution)/shard_map/ppermute | solution.py:208
  251.8 6.7 %collective-permute-start.23 = (bf16[128,256]{1,0:T(8,128)(2,1)S(1)}, bf16[128,256]{1,0:T(8,128)(2,1)S(1)}, u32[]{:S(2)}, u32[]{:S(2)}) collective-permute-start(bf16[128,256]{1,0:T(8,128)(2,1)S(1)} %get-tuple-element.17), channel_id=1, source_target_pairs={{0,192},{64,0},{128,64},{192,128},{1,193},{65,1},{129,65},{193,129... | collective-permute-start | bytes 196616 | tf_op jit(solution)/shard_map/ppermute | solution.py:211
  254.0 7.1 %collective-permute-start.24 = (bf16[128,256]{1,0:T(8,128)(2,1)S(1)}, bf16[128,256]{1,0:T(8,128)(2,1)S(1)}, u32[]{:S(2)}, u32[]{:S(2)}) collective-permute-start(bf16[128,256]{1,0:T(8,128)(2,1)S(1)} %get-tuple-element.18), channel_id=1, source_target_pairs={{0,128},{64,192},{128,0},{192,64},{1,129},{65,193},{129,1},{193,65... | collective-permute-start | bytes 196616 | tf_op jit(solution)/shard_map/ppermute | solution.py:211
  258.5 5.8 %collective-permute-start.25 = (bf16[128,256]{1,0:T(8,128)(2,1)S(1)}, bf16[128,256]{1,0:T(8,128)(2,1)S(1)}, u32[]{:S(2)}, u32[]{:S(2)}) collective-permute-start(bf16[128,256]{1,0:T(8,128)(2,1)S(1)} %get-tuple-element.19), channel_id=1, source_target_pairs={{0,64},{64,128},{128,192},{192,0},{1,65},{65,129},{129,193},{193,1... | collective-permute-start | bytes 196616 | tf_op jit(solution)/shard_map/ppermute | solution.py:211
  264.2 3.4 %copy-start = (bf16[1024,4096]{1,0:T(8,128)(2,1)S(1)}, bf16[1024,4096]{1,0:T(8,128)(2,1)}, u32[]{:S(2)}) copy-start(bf16[1024,4096]{1,0:T(8,128)(2,1)} %all-gather.2.cloned.1.call-done.refs_4_) | copy-start | bytes 25165828
  267.6 7.1 %copy-start.1 = (bf16[64,4096]{1,0:T(8,128)(2,1)S(1)}, bf16[64,4096]{1,0:T(8,128)(2,1)}, u32[]{:S(2)}) copy-start(bf16[64,4096]{1,0:T(8,128)(2,1)} %residual.1) | copy-start | bytes 1572868
  267.6 7.1 %copy-start.2 = (f32[4096]{0:T(1024)S(1)}, f32[4096]{0:T(1024)}, u32[]{:S(2)}) copy-start(f32[4096]{0:T(1024)} %param.13) | copy-start | bytes 49156
  269.5 5.2 %collective-permute-start.29 = (f32[64,4096]{1,0:T(8,128)S(1)}, f32[64,4096]{1,0:T(8,128)S(1)}, u32[]{:S(2)}, u32[]{:S(2)}) collective-permute-start(f32[64,4096]{1,0:T(8,128)S(1)} %get-tuple-element.21), channel_id=1, source_target_pairs={{0,1},{1,0},{2,3},{3,2},{4,5},{5,4},{6,7},{7,6},{8,9},{9,8},{10,11... | collective-permute-start | bytes 3145736 | tf_op jit(solution)/shard_map/ppermute | solution.py:26
Sparse Core Ops, SparseCore 0:
  27.3 106.9 all-gather.1
where the time goes:
time: 284 us; the launch traced here: 283 us
  waiting for transfers between devices  130 us (46%)
  starting transfers between devices  103 us (36%)
  Pallas kernels  18.6 us (7%)
  between operations  14.2 us (5%)
  local copies, waits for them, and re-layouts  11.7 us (4%)
  other arithmetic  5.68 us (2%)
    ppermute x9, starting transfers between devices, swap(): return lax.ppermute(a, axis, [(0, 1), (1, 0)])  53.3 us
    ppermute x9, waiting for transfers between devices, swap(): return lax.ppermute(a, axis, [(0, 1), (1, 0)])  33 us
    ppermute x1, waiting for transfers between devices, shards(): w_prev = lax.ppermute(w_near, Y, FWD)  26.1 us
    ppermute x6, waiting for transfers between devices, beyond(): lax.ppermute(a, axis, [(i, (i + 4 - d) % 4) for i in range(4)])  25.2 us
    pallas_call x5, Pallas kernels, kernel_call(): pl.pallas_call(kernel, out_shape=outs, in_specs=[pl.BlockSpec(memory_spac...  18.6 us
    ppermute x1, waiting for transfers between devices, shards(): w_far_a = lax.ppermute(w_prev[:2], Y, FWD)  14.6 us
    ppermute x6, starting transfers between devices, beyond(): lax.ppermute(a, axis, [(i, (i + 4 - d) % 4) for i in range(4)])  13.9 us
    all_to_all x1, starting transfers between devices, shards(): lax.all_to_all(both.reshape(16, 64, 512), (X, 'yh', 'c'), 0, 0, tiled=True)  10.7 us
  transfers between devices with their start and end apart: 32, of which 21 were waited for; matrix products, arithmetic and copies ran while one was open for 4% of the time, Pallas kernels for 5%

commit v1 on v0

--- a/solution.py
+++ b/solution.py
@@ -15,7 +15,6 @@
 F32 = jnp.float32
 X = "x"
 Y = ("yh", "yl")
-XY = ("x", "yh", "yl")
 Z = "zh"
 EXP_SCALE = math.log2(math.e) / math.sqrt(DH)
 FWD = [(i, (i + 1) % 4) for i in range(4)]
@@ -100,7 +99,6 @@
 
 
 def merge_kernel(where_ref, a_ref, b_ref, c_ref, d_ref, *outs):
-    zh = where_ref[0]
     refs = (a_ref, b_ref, c_ref, d_ref)
     contexts = []
     for side in range(2):
@@ -111,44 +109,48 @@
         inverse = 1.0 / sum(weight)
         context = sum(ref[side, :DH].astype(F32) * (w * inverse) for ref, w in zip(refs, weight))
         contexts.append(context.T.astype(BF))
-    for d in range(4):
-        for m in range(4):
-
-            @pl.when(lax.rem(zh + d, 4) == m)
-            def _(d=d, m=m):
-                for side in range(2):
-                    outs[d][side * 64 : (side + 1) * 64] = contexts[side][m * 64 : (m + 1) * 64]
+    c = where_ref[3]
+    outs[0][...] = jnp.where(c == 0, contexts[0], contexts[1])
+    outs[1][...] = jnp.where(c == 0, contexts[1], contexts[0])
 
 
 def merge(where, parts):
-    return kernel_call(merge_kernel, [jax.ShapeDtypeStruct((128, DH), BF)] * 4, where, *parts)
-
-
-def output_kernel(where_ref, *refs):
-    c = where_ref[3]
-    w_ref, out_mine, out_theirs = refs[4:]
-    rows = jnp.concatenate([ref[...] for ref in refs[:4]], 1)
+    return kernel_call(merge_kernel, [jax.ShapeDtypeStruct((256, DH), BF)] * 2, where, *parts)
+
+
+def output_kernel(where_ref, mine, theirs, w_ref, own, fwd_a, fwd_b, bwd_a, bwd_b, far_a, far_b):
+    zh, c = where_ref[0], where_ref[3]
+
+    def by_distance(ref):
+        return jnp.concatenate([ref[pl.ds(pl.multiple_of(lax.rem(zh + d, 4) * 64, 64), 64)] for d in range(4)], 0)
+
+    rows = (by_distance(mine), by_distance(theirs))
+    heads = [pl.ds(pl.multiple_of(h * DH, DH), DH) for h in (c, 1 - c)]
     for i in range(8):
         cols = slice(i * 512, (i + 1) * 512)
-        acc = jnp.dot(rows, w_ref[:, cols], preferred_element_type=F32)
-        low, high = acc[:64], acc[64:]
-        out_mine[:, cols] = jnp.where(c == 0, low, high)
-        out_theirs[:, cols] = jnp.where(c == 0, high, low)
-
-
-def output(where, ctx, w):
-    return kernel_call(output_kernel, [jax.ShapeDtypeStruct((64, 4096), F32)] * 2, where, *ctx, w)
-
-
-def finish_kernel(where_ref, mine, other, residual, gain, hidden, normed):
-    x = residual[...].astype(F32) + (mine[...] + other[...])
-    scale = lax.rsqrt(jnp.mean(x * x, -1, keepdims=True) + 1e-06)
-    hidden[...] = x.astype(BF)
-    normed[...] = (x * scale * gain[...]).astype(BF)
+        acc = sum(jnp.dot(r, w_ref[h, cols], preferred_element_type=F32) for r, h in zip(rows, heads))
+        own[:, cols] = acc[:64]
+        for at, out in ((64, fwd_a), (96, fwd_b), (128, far_a), (160, far_b), (192, bwd_a), (224, bwd_b)):
+            out[:, cols] = acc[at : at + 32].astype(out.dtype)
+
+
+def output(where, mine, theirs, w):
+    outs = [jax.ShapeDtypeStruct((64, 4096), F32)]
+    outs += [jax.ShapeDtypeStruct((32, 4096), t) for t in (F32, BF, BF, F32, BF, BF)]
+    return kernel_call(output_kernel, outs, where, mine, theirs, w)
+
+
+def finish_kernel(where_ref, own, prev_a, prev_b, next_a, next_b, residual, gain, hidden, normed):
+    for at, left, right in ((0, prev_a, next_a), (32, prev_b, next_b)):
+        rows = slice(at, at + 32)
+        x = residual[rows].astype(F32) + (own[rows] + (left[...].astype(F32) + right[...].astype(F32)))
+        scale = lax.rsqrt(jnp.mean(x * x, -1, keepdims=True) + 1e-06)
+        hidden[rows] = x.astype(BF)
+        normed[rows] = (x * scale * gain[...]).astype(BF)
 
 
 def finish(where, *args):
-    return kernel_call(finish_kernel, [jax.ShapeDtypeStruct(args[2].shape, BF)] * 2, where, *args)
+    return kernel_call(finish_kernel, [jax.ShapeDtypeStruct((64, 4096), BF)] * 2, where, *args)
 
 
 def shards(memory, kv_weight, mem_lengths, queries, out_weight, residual, norm_gain):
@@ -180,12 +182,6 @@
     far_b = lax.ppermute(next_b, Z, BWD)
     pieces = (mem_a, mem_b, next_a, next_b, far_a, far_b, prev_a, prev_b)
 
-    ow = lax.dynamic_slice(out_weight, (c * DH, (x * 4 + y) * 256), (DH, 256))
-    ow = [ow, *beyond(ow, Z)]
-    ow = jnp.concatenate(ow, 0)
-
-    ow = lax.all_gather(ow, XY, axis=1, tiled=True)
-
     other = pick(queries[:, DH:], queries[:, :DH], c)
     other = swap(other, "c")
     q = pair(pick(queries[:, :DH], queries[:, DH:], c), other, c)
@@ -207,10 +203,18 @@
         swap(to_yl, "yl"),
         lax.ppermute(to_both, ("yl", "zl"), [(i, 3 - i) for i in range(4)]),
     )
-    pieces = merge(where, parts)
-    ctx = [pieces[0]] + [lax.ppermute(pieces[4 - d], Z, [(i, (i + 4 - d) % 4) for i in range(4)]) for d in (1, 2, 3)]
-    mine, theirs = output(where, ctx, ow)
-    return tuple(finish(where, mine, swap(theirs, "c"), residual, norm_gain.reshape(1, -1)))
+    mine, theirs = merge(where, parts)
+    own, fwd_a, fwd_b, bwd_a, bwd_b, far_a, far_b = output(where, mine, swap(theirs, "c"), out_weight)
+
+    far_a = lax.ppermute(far_a, Z, FWD)
+    far_b = lax.ppermute(far_b, Z, BWD)
+    prev_b = lax.ppermute(fwd_b, Z, FWD)
+    next_a = lax.ppermute(bwd_a, Z, BWD)
+    fwd_a = (fwd_a + far_a.astype(F32)).astype(BF)
+    bwd_b = (bwd_b + far_b.astype(F32)).astype(BF)
+    prev_a = lax.ppermute(fwd_a, Z, FWD)
+    next_b = lax.ppermute(bwd_b, Z, BWD)
+    return tuple(finish(where, own, prev_a, prev_b, next_a, next_b, residual, norm_gain.reshape(1, -1)))
 
 
 def solution(mesh):

time: 284 us -> 255 us (0.90)
  starting transfers between devices: 103 us -> 57.1 us
  waiting for transfers between devices: 130 us -> 163 us
  between operations: 14.2 us -> 0.84 us
    ppermute x9, starting transfers between devices: 53.3 us -> 24.7 us  [swap(): return lax.ppermute(a, axis, [(0, 1), (1, 0)])]
    ppermute x3 -> x6, waiting for transfers between devices: 5.75 us -> 28.5 us  [the longest x1 19.9 us: shards(): far_b = lax.ppermute(far_b, Z, BWD)]
    ppermute x1, waiting for transfers between devices: 0.85 us -> 18.9 us  [shards(): next_b = lax.ppermute(mem_b, Z, BWD)]
    ppermute x6 -> x3, starting transfers between devices: 13.9 us -> 1.8 us  [beyond(): lax.ppermute(a, axis, [(i, (i + 4 - d) % 4) for i in range(4)])]
    ppermute x6 -> x3, waiting for transfers between devices: 25.2 us -> 13.4 us  [beyond(): lax.ppermute(a, axis, [(i, (i + 4 - d) % 4) for i in range(4)])]
    ppermute x1, waiting for transfers between devices: 0.01 us -> 10.2 us  [shards(): far_b = lax.ppermute(next_b, Z, BWD)]
    ppermute x1, waiting for transfers between devices: 14.6 us -> 8.06 us  [shards(): w_far_a = lax.ppermute(w_prev[:2], Y, FWD)]
    all_to_all x1, starting transfers between devices: 10.7 us -> 4.29 us  [shards(): lax.all_to_all(both.reshape(16, 64, 512), (X, 'yh', 'c'), 0, 0, tiled=True)]
  transfers between devices with their start and end apart: 32 -> 31, of which waited for: 21 -> 21; matrix products, arithmetic and copies ran while one was open for 4% -> 4% of each run, Pallas kernels for 5% -> 4%
where the time goes in v1:
time: 255 us; the launch traced here: 254 us
  waiting for transfers between devices  163 us (64%)
  starting transfers between devices  57.1 us (22%)
  Pallas kernels  18.3 us (7%)
  local copies, waits for them, and re-layouts  9.69 us (4%)
  other arithmetic  5.02 us (2%)
    ppermute x9, waiting for transfers between devices, swap(): return lax.ppermute(a, axis, [(0, 1), (1, 0)])  35.4 us
    ppermute x9, starting transfers between devices, swap(): return lax.ppermute(a, axis, [(0, 1), (1, 0)])  24.7 us
    ppermute x1, waiting for transfers between devices, shards(): w_prev = lax.ppermute(w_near, Y, FWD)  22 us
    ppermute x1, waiting for transfers between devices, shards(): far_b = lax.ppermute(far_b, Z, BWD)  19.9 us
    ppermute x1, waiting for transfers between devices, shards(): next_b = lax.ppermute(mem_b, Z, BWD)  18.9 us
    pallas_call x5, Pallas kernels, kernel_call(): pl.pallas_call(kernel, out_shape=outs, in_specs=[pl.BlockSpec(memory_spac...  18.3 us
    ppermute x3, waiting for transfers between devices, beyond(): lax.ppermute(a, axis, [(i, (i + 4 - d) % 4) for i in range(4)])  13.4 us
    ppermute x1, waiting for transfers between devices, shards(): prev_a = lax.ppermute(mem_a, Z, FWD)  12.4 us
  transfers between devices with their start and end apart: 31, of which 21 were waited for; matrix products, arithmetic and copies ran while one was open for 4% of the time, Pallas kernels for 4%

profile of v1, /device:TPU:1, one launch (start us, length us, event | category | flops | bytes accessed | tf_op | source)
XLA Modules:
  0.0 254.1 jit_solution(4624057165727605977)
XLA Ops:
  1.5 3.3 %collective-permute-start.9 = (bf16[64,512]{1,0:T(8,128)(2,1)S(1)}, bf16[64,512]{1,0:T(8,128)(2,1)S(1)}, u32[]{:S(2)}, u32[]{:S(2)}) collective-permute-start(bf16[64,512]{1,0:T(8,128)(2,1)S(1)} %get-tuple-element.35), channel_id=1, source_target_pairs={{0,1},{1,0},{2,3},{3,2},{4,5},{5,4},{6,7},{7,6},{8,9},{9,8},{10,11... | collective-permute-start | bytes 196616 | tf_op jit(solution)/shard_map/ppermute | solution.py:25
  4.8 1.4 collective-permute-start.10
  6.3 3.4 %collective-permute-done.10 = bf16[64,512]{1,0:T(8,128)(2,1)S(1)} collective-permute-done((bf16[64,512]{1,0:T(8,128)(2,1)S(1)}, bf16[64,512]{1,0:T(8,128)(2,1)S(1)}, u32[]{:S(2)}, u32[]{:S(2)}) %collective-permute-start.10) | collective-permute-done | bytes 65568 | tf_op jit(solution)/shard_map/ppermute | solution.py:25
  12.4 4.4 %collective-permute-done.12 = bf16[256,512]{1,0:T(8,128)(2,1)S(1)} collective-permute-done((bf16[256,512]{1,0:T(8,128)(2,1)S(1)}, bf16[256,512]{1,0:T(8,128)(2,1)S(1)}, u32[]{:S(2)}, u32[]{:S(2)}) %collective-permute-start.12) | collective-permute-done | bytes 262176 | tf_op jit(solution)/shard_map/ppermute | solution.py:29
  16.8 1.3 collective-permute-done.13
  18.1 7.7 %collective-permute-done.14 = bf16[256,512]{1,0:T(8,128)(2,1)S(1)} collective-permute-done((bf16[256,512]{1,0:T(8,128)(2,1)S(1)}, bf16[256,512]{1,0:T(8,128)(2,1)S(1)}, u32[]{:S(2)}, u32[]{:S(2)}) %collective-permute-start.14) | collective-permute-done | bytes 262176 | tf_op jit(solution)/shard_map/ppermute | solution.py:29
  26.0 1.4 collective-permute-start.16
  27.4 1.5 collective-permute-start.15
  29.6 22.0 %collective-permute-done.16 = bf16[4,256,512]{2,1,0:T(8,128)(2,1)S(1)} collective-permute-done((bf16[4,256,512]{2,1,0:T(8,128)(2,1)S(1)}, bf16[4,256,512]{2,1,0:T(8,128)(2,1)S(1)}, u32[]{:S(2)}, u32[]{:S(2)}) %collective-permute-start.16) | collective-permute-done | bytes 1048608 | tf_op jit(solution)/shard_map/ppermute | solution.py:169
  51.8 2.7 %collective-permute-start.18 = (bf16[2,256,512]{2,1,0:T(8,128)(2,1)S(1)}, bf16[2,256,512]{2,1,0:T(8,128)(2,1)S(1)}, u32[]{:S(2)}, u32[]{:S(2)}) collective-permute-start(bf16[2,256,512]{2,1,0:T(8,128)(2,1)S(1)} %slice.37), channel_id=1, source_target_pairs={{0,12},{4,0},{8,4},{12,8},{1,13},{5,1},{9,5},{13,9},{2,14},{6,2},{... | collective-permute-start | bytes 1572872 | tf_op jit(solution)/shard_map/ppermute | solution.py:172
  56.0 1.1 constant_dynamic-update-slice_fusion.3
  57.1 8.1 %collective-permute-done.17 = bf16[2,256,512]{2,1,0:T(8,128)(2,1)S(1)} collective-permute-done((bf16[2,256,512]{2,1,0:T(8,128)(2,1)S(1)}, bf16[2,256,512]{2,1,0:T(8,128)(2,1)S(1)}, u32[]{:S(2)}, u32[]{:S(2)}) %collective-permute-start.17) | collective-permute-done | bytes 524320 | tf_op jit(solution)/shard_map/ppermute | solution.py:171
  66.8 1.1 constant_dynamic-update-slice_fusion
  67.9 2.1 collective-permute-start.19
  70.2 3.1 %collective-permute-start.5 = (bf16[256,1024]{1,0:T(8,128)(2,1)S(1)}, bf16[256,1024]{1,0:T(8,128)(2,1)S(1)}, u32[]{:S(2)}, u32[]{:S(2)}) collective-permute-start(bf16[256,1024]{1,0:T(8,128)(2,1)S(1)} %bitcast.27), channel_id=1, source_target_pairs={{0,64},{64,128},{128,192},{192,0},{1,65},{65,129},{129,193},{193,1... | collective-permute-start | bytes 1572872 | tf_op jit(solution)/shard_map/ppermute | solution.py:177
  73.2 3.3 %collective-permute-start.4 = (bf16[256,1024]{1,0:T(8,128)(2,1)S(1)}, bf16[256,1024]{1,0:T(8,128)(2,1)S(1)}, u32[]{:S(2)}, u32[]{:S(2)}) collective-permute-start(bf16[256,1024]{1,0:T(8,128)(2,1)S(1)} %bitcast.24), channel_id=1, source_target_pairs={{0,192},{64,0},{128,64},{192,128},{1,193},{65,1},{129,65},{193,129... | collective-permute-start | bytes 1572872 | tf_op jit(solution)/shard_map/ppermute | solution.py:179
  76.5 2.3 collective-permute-start.3
  79.7 1.0 collective-permute-done
  80.7 12.4 %collective-permute-done.5.refs_6_ = bf16[256,1024]{1,0:T(8,128)(2,1)S(1)} collective-permute-done((bf16[256,1024]{1,0:T(8,128)(2,1)S(1)}, bf16[256,1024]{1,0:T(8,128)(2,1)S(1)}, u32[]{:S(2)}, u32[]{:S(2)}) %collective-permute-start.5) | collective-permute-done | bytes 524320 | tf_op jit(solution)/shard_map/ppermute | solution.py:177
  93.3 18.9 %collective-permute-done.4.refs_3_ = bf16[256,1024]{1,0:T(8,128)(2,1)S(1)} collective-permute-done((bf16[256,1024]{1,0:T(8,128)(2,1)S(1)}, bf16[256,1024]{1,0:T(8,128)(2,1)S(1)}, u32[]{:S(2)}, u32[]{:S(2)}) %collective-permute-start.4) | collective-permute-done | bytes 524320 | tf_op jit(solution)/shard_map/ppermute | solution.py:179
  112.2 2.4 collective-permute-start.7
  114.7 8.8 %collective-permute-done.3.refs_2_ = bf16[256,1024]{1,0:T(8,128)(2,1)S(1)} collective-permute-done((bf16[256,1024]{1,0:T(8,128)(2,1)S(1)}, bf16[256,1024]{1,0:T(8,128)(2,1)S(1)}, u32[]{:S(2)}, u32[]{:S(2)}) %collective-permute-start.3) | collective-permute-done | bytes 524320 | tf_op jit(solution)/shard_map/ppermute | solution.py:178
  123.6 1.1 collective-permute-done.6.refs_4_
  124.7 10.2 %collective-permute-done.7.refs_5_ = bf16[256,1024]{1,0:T(8,128)(2,1)} collective-permute-done((bf16[256,1024]{1,0:T(8,128)(2,1)S(1)}, bf16[256,1024]{1,0:T(8,128)(2,1)}, u32[]{:S(2)}, u32[]{:S(2)}) %collective-permute-start.7) | collective-permute-done | bytes 524320 | tf_op jit(solution)/shard_map/ppermute | solution.py:182
  134.9 9.3 %shard_map.86 = bf16[8,2,64,512]{3,2,1,0:T(8,128)(2,1)} custom-call(s32[4]{0:T(128)S(1)} %pad_add_fusion.where_ref, bf16[256,1024]{1,0:T(8,128)(2,1)S(1)} %bitcast.29, bf16[256,1024]{1,0:T(8,128)(2,1)S(1)} %bitcast.26, bf16[256,1024]{1,0:T(8,128)(2,1)S(1)} %collective-permute-done.3.refs_2_, bf16[256,1024]{1,0:T(8,128)(2,1)S(1)} %collective-permute-done.4.refs_3_, ...), custom_call_target="tpu_custom_call" | custom-call | tf_op jit(solution)/shard_map/pallas_call | solution.py:43
  144.1 4.3 %all-to-all-start = ((bf16[16,64,512]{2,1,0:T(8,128)(2,1)}), bf16[16,64,512]{2,1,0:T(8,128)(2,1)S(1)}, u32[]{:S(2)}, u32[]{:S(2)}) async-start(bf16[16,64,512]{2,1,0:T(8,128)(2,1)} %bitcast.17), calls=%async_computation | async-start | bytes 2097152 | tf_op jit(solution)/shard_map/all_to_all | solution.py:197
  148.4 3.5 %collective-permute-done.1 = bf16[512,256]{1,0:T(8,128)(2,1)} collective-permute-done((bf16[512,256]{1,0:T(8,128)(2,1)S(1)}, bf16[512,256]{1,0:T(8,128)(2,1)}, u32[]{:S(2)}, u32[]{:S(2)}) %collective-permute-start.1) | collective-permute-done | bytes 262176 | tf_op jit(solution)/shard_map/ppermute | solution.py:25
  151.9 1.2 maximum_select_fusion.1
  154.6 19.7 %collective-permute-done.2 = bf16[1024,256]{1,0:T(8,128)(2,1)} collective-permute-done((bf16[1024,256]{1,0:T(8,128)(2,1)S(1)}, bf16[1024,256]{1,0:T(8,128)(2,1)}, u32[]{:S(2)}, u32[]{:S(2)}) %collective-permute-start.2) | collective-permute-done | bytes 524320 | tf_op jit(solution)/shard_map/ppermute | solution.py:25
  174.2 1.6 maximum_select_fusion.q_ref
  175.8 4.5 %shard_map.87 = (bf16[2,272,256]{2,1,0:T(8,128)(2,1)S(1)}, bf16[2,272,256]{2,1,0:T(8,128)(2,1)S(1)}, bf16[2,272,256]{2,1,0:T(8,128)(2,1)S(1)}, bf16[2,272,256]{2,1,0:T(8,128)(2,1)S(1)}) custom-call(s32[6]{0:T(128)S(1)} %stack.57.where_ref, bf16[2048,256]{1,0:T(8,128)(2,1)S(1)} %maximum_select_fusion.q_ref, bf16[1024,512]{1,0:T(8,128)(2,1)S(1)} %bitcast.23), custom_call_target="tpu_custom_call" | custom-call | tf_op jit(solution)/shard_map/pallas_call | solution.py:43
  180.3 13.5 %collective-permute-start.20 = (bf16[2,272,256]{2,1,0:T(8,128)(2,1)S(1)}, bf16[2,272,256]{2,1,0:T(8,128)(2,1)S(1)}, u32[]{:S(2)}, u32[]{:S(2)}) collective-permute-start(bf16[2,272,256]{2,1,0:T(8,128)(2,1)S(1)} %get-tuple-element.16), channel_id=1, source_target_pairs={{0,2},{2,0},{1,3},{3,1},{4,6},{6,4},{5,7},{7,5},{8,10},{10,8},{9,1... | collective-permute-start | bytes 835592 | tf_op jit(solution)/shard_map/ppermute | solution.py:25
  195.1 5.1 %collective-permute-done.20.b_ref = bf16[2,272,256]{2,1,0:T(8,128)(2,1)S(1)} collective-permute-done((bf16[2,272,256]{2,1,0:T(8,128)(2,1)S(1)}, bf16[2,272,256]{2,1,0:T(8,128)(2,1)S(1)}, u32[]{:S(2)}, u32[]{:S(2)}) %collective-permute-start.20) | collective-permute-done | bytes 278560 | tf_op jit(solution)/shard_map/ppermute | solution.py:25
  200.3 1.8 collective-permute-done.21.c_ref
  202.0 4.3 %collective-permute-done.22.d_ref = bf16[2,272,256]{2,1,0:T(8,128)(2,1)S(1)} collective-permute-done((bf16[2,272,256]{2,1,0:T(8,128)(2,1)S(1)}, bf16[2,272,256]{2,1,0:T(8,128)(2,1)S(1)}, u32[]{:S(2)}, u32[]{:S(2)}) %collective-permute-start.22) | collective-permute-done | bytes 278560 | tf_op jit(solution)/shard_map/ppermute | solution.py:204
  207.2 2.9 %collective-permute-start.23 = (bf16[256,256]{1,0:T(8,128)(2,1)S(1)}, bf16[256,256]{1,0:T(8,128)(2,1)S(1)}, u32[]{:S(2)}, u32[]{:S(2)}) collective-permute-start(bf16[256,256]{1,0:T(8,128)(2,1)S(1)} %get-tuple-element.20), channel_id=1, source_target_pairs={{0,1},{1,0},{2,3},{3,2},{4,5},{5,4},{6,7},{7,6},{8,9},{9,8},{10,11... | collective-permute-start | bytes 393224 | tf_op jit(solution)/shard_map/ppermute | solution.py:25
  210.1 1.0 collective-permute-done.23.theirs
  211.1 2.2 copy-done
  213.2 1.8 shard_map.89
  215.3 2.2 collective-permute-start.24
  217.5 1.7 collective-permute-start.26
  219.2 1.8 collective-permute-start.27
  221.1 19.9 %collective-permute-done.28 = bf16[32,4096]{1,0:T(8,128)(2,1)S(1)} collective-permute-done((bf16[32,4096]{1,0:T(8,128)(2,1)S(1)}, bf16[32,4096]{1,0:T(8,128)(2,1)S(1)}, u32[]{:S(2)}, u32[]{:S(2)}) %collective-permute-start.28) | collective-permute-done | bytes 262176 | tf_op jit(solution)/shard_map/ppermute | solution.py:210
  241.0 1.5 collective-permute-start.29
  242.6 1.0 collective-permute-start.25
  243.6 3.0 %collective-permute-done.27.next_a = bf16[32,4096]{1,0:T(8,128)(2,1)S(1)} collective-permute-done((bf16[32,4096]{1,0:T(8,128)(2,1)S(1)}, bf16[32,4096]{1,0:T(8,128)(2,1)S(1)}, u32[]{:S(2)}, u32[]{:S(2)}) %collective-permute-start.27) | collective-permute-done | bytes 262176 | tf_op jit(solution)/shard_map/ppermute | solution.py:212
  246.6 5.6 %collective-permute-done.29.next_b = bf16[32,4096]{1,0:T(8,128)(2,1)S(1)} collective-permute-done((bf16[32,4096]{1,0:T(8,128)(2,1)S(1)}, bf16[32,4096]{1,0:T(8,128)(2,1)S(1)}, u32[]{:S(2)}, u32[]{:S(2)}) %collective-permute-start.29) | collective-permute-done | bytes 262176 | tf_op jit(solution)/shard_map/ppermute | solution.py:216
  252.2 1.9 shard_map.90
  (56 shorter events, 13.1 us)
Async XLA Ops:
  1.5 4.7 %collective-permute-start.9 = (bf16[64,512]{1,0:T(8,128)(2,1)S(1)}, bf16[64,512]{1,0:T(8,128)(2,1)S(1)}, u32[]{:S(2)}, u32[]{:S(2)}) collective-permute-start(bf16[64,512]{1,0:T(8,128)(2,1)S(1)} %get-tuple-element.35), channel_id=1, source_target_pairs={{0,1},{1,0},{2,3},{3,2},{4,5},{5,4},{6,7},{7,6},{8,9},{9,8},{10,11... | collective-permute-start | bytes 196616 | tf_op jit(solution)/shard_map/ppermute | solution.py:25
  4.8 4.9 %collective-permute-start.11 = (bf16[64,512]{1,0:T(8,128)(2,1)S(1)}, bf16[64,512]{1,0:T(8,128)(2,1)S(1)}, u32[]{:S(2)}, u32[]{:S(2)}) collective-permute-start(bf16[64,512]{1,0:T(8,128)(2,1)S(1)} %get-tuple-element.35), channel_id=1, source_target_pairs={{0,3},{1,2},{2,1},{3,0},{4,7},{5,6},{6,5},{7,4},{8,11},{9,10},{10,... | collective-permute-start | bytes 196616 | tf_op jit(solution)/shard_map/ppermute | solution.py:165
  4.8 4.9 %collective-permute-start.10 = (bf16[64,512]{1,0:T(8,128)(2,1)S(1)}, bf16[64,512]{1,0:T(8,128)(2,1)S(1)}, u32[]{:S(2)}, u32[]{:S(2)}) collective-permute-start(bf16[64,512]{1,0:T(8,128)(2,1)S(1)} %get-tuple-element.34), channel_id=1, source_target_pairs={{0,2},{2,0},{1,3},{3,1},{4,6},{6,4},{5,7},{7,5},{8,10},{10,8},{9,1... | collective-permute-start | bytes 196616 | tf_op jit(solution)/shard_map/ppermute | solution.py:25
  9.8 7.0 %collective-permute-start.12 = (bf16[256,512]{1,0:T(8,128)(2,1)S(1)}, bf16[256,512]{1,0:T(8,128)(2,1)S(1)}, u32[]{:S(2)}, u32[]{:S(2)}) collective-permute-start(bf16[256,512]{1,0:T(8,128)(2,1)S(1)} %maximum_select_fusion.4), channel_id=1, source_target_pairs={{0,48},{16,0},{32,16},{48,32},{1,49},{17,1},{33,17},{49,33},{2,50}... | collective-permute-start | bytes 786440 | tf_op jit(solution)/shard_map/ppermute | solution.py:29
  10.5 7.6 %collective-permute-start.13 = (bf16[256,512]{1,0:T(8,128)(2,1)S(1)}, bf16[256,512]{1,0:T(8,128)(2,1)S(1)}, u32[]{:S(2)}, u32[]{:S(2)}) collective-permute-start(bf16[256,512]{1,0:T(8,128)(2,1)S(1)} %maximum_select_fusion.4), channel_id=1, source_target_pairs={{0,32},{16,48},{32,0},{48,16},{1,33},{17,49},{33,1},{49,17},{2,34}... | collective-permute-start | bytes 786440 | tf_op jit(solution)/shard_map/ppermute | solution.py:29
  11.0 14.8 %collective-permute-start.14 = (bf16[256,512]{1,0:T(8,128)(2,1)S(1)}, bf16[256,512]{1,0:T(8,128)(2,1)S(1)}, u32[]{:S(2)}, u32[]{:S(2)}) collective-permute-start(bf16[256,512]{1,0:T(8,128)(2,1)S(1)} %maximum_select_fusion.4), channel_id=1, source_target_pairs={{0,16},{16,32},{32,48},{48,0},{1,17},{17,33},{33,49},{49,1},{2,18}... | collective-permute-start | bytes 786440 | tf_op jit(solution)/shard_map/ppermute | solution.py:29
  26.0 25.6 %collective-permute-start.16 = (bf16[4,256,512]{2,1,0:T(8,128)(2,1)S(1)}, bf16[4,256,512]{2,1,0:T(8,128)(2,1)S(1)}, u32[]{:S(2)}, u32[]{:S(2)}) collective-permute-start(bf16[4,256,512]{2,1,0:T(8,128)(2,1)S(1)} %pad_maximum_fusion), channel_id=1, source_target_pairs={{0,4},{4,8},{8,12},{12,0},{1,5},{5,9},{9,13},{13,1},{2,6},{6,10},{... | collective-permute-start | bytes 3145736 | tf_op jit(solution)/shard_map/ppermute | solution.py:169
  27.4 24.4 %collective-permute-start.15 = (bf16[4,256,512]{2,1,0:T(8,128)(2,1)S(1)}, bf16[4,256,512]{2,1,0:T(8,128)(2,1)S(1)}, u32[]{:S(2)}, u32[]{:S(2)}) collective-permute-start(bf16[4,256,512]{2,1,0:T(8,128)(2,1)S(1)} %pad_maximum_fusion), channel_id=1, source_target_pairs={{0,12},{4,0},{8,4},{12,8},{1,13},{5,1},{9,5},{13,9},{2,14},{6,2},{... | collective-permute-start | bytes 3145736 | tf_op jit(solution)/shard_map/ppermute | solution.py:170
  51.7 18.4 %copy-start.3 = (bf16[8,64,1024]{2,1,0:T(8,128)(2,1)S(1)}, bf16[8,64,1024]{2,1,0:T(8,128)(2,1)}, u32[]{:S(2)}) copy-start(bf16[8,64,1024]{2,1,0:T(8,128)(2,1)} %param.7) | copy-start | bytes 3145732
  51.7 13.5 %collective-permute-start.17 = (bf16[2,256,512]{2,1,0:T(8,128)(2,1)S(1)}, bf16[2,256,512]{2,1,0:T(8,128)(2,1)S(1)}, u32[]{:S(2)}, u32[]{:S(2)}) collective-permute-start(bf16[2,256,512]{2,1,0:T(8,128)(2,1)S(1)} %slice.36), channel_id=1, source_target_pairs={{0,4},{4,8},{8,12},{12,0},{1,5},{5,9},{9,13},{13,1},{2,6},{6,10},{... | collective-permute-start | bytes 1572872 | tf_op jit(solution)/shard_map/ppermute | solution.py:171
  51.8 14.2 %collective-permute-start.18 = (bf16[2,256,512]{2,1,0:T(8,128)(2,1)S(1)}, bf16[2,256,512]{2,1,0:T(8,128)(2,1)S(1)}, u32[]{:S(2)}, u32[]{:S(2)}) collective-permute-start(bf16[2,256,512]{2,1,0:T(8,128)(2,1)S(1)} %slice.37), channel_id=1, source_target_pairs={{0,12},{4,0},{8,4},{12,8},{1,13},{5,1},{9,5},{13,9},{2,14},{6,2},{... | collective-permute-start | bytes 1572872 | tf_op jit(solution)/shard_map/ppermute | solution.py:172
  56.0 22.8 %copy-start.4 = (bf16[256,512]{1,0:T(8,128)(2,1)S(1)}, bf16[256,512]{1,0:T(8,128)(2,1)}, u32[]{:S(2)}) copy-start(bf16[256,512]{1,0:T(8,128)(2,1)} %param.10) | copy-start | bytes 786436
  67.9 66.9 %collective-permute-start.19 = (bf16[4,4,256,512]{3,2,1,0:T(8,128)(2,1)}, bf16[4,4,256,512]{3,2,1,0:T(8,128)(2,1)}, u32[]{:S(2)}, u32[]{:S(2)}) collective-permute-start(bf16[4,4,256,512]{3,2,1,0:T(8,128)(2,1)} %bitcast.16.refs_8_), channel_id=1, source_target_pairs={{0,1},{1,0},{2,3},{3,2},{4,5},{5,4},{6,7},{7,6},{8,9},{9,8},{10,11... | collective-permute-start | bytes 12582920 | tf_op jit(solution)/shard_map/ppermute | solution.py:25
  70.2 23.0 %collective-permute-start.5 = (bf16[256,1024]{1,0:T(8,128)(2,1)S(1)}, bf16[256,1024]{1,0:T(8,128)(2,1)S(1)}, u32[]{:S(2)}, u32[]{:S(2)}) collective-permute-start(bf16[256,1024]{1,0:T(8,128)(2,1)S(1)} %bitcast.27), channel_id=1, source_target_pairs={{0,64},{64,128},{128,192},{192,0},{1,65},{65,129},{129,193},{193,1... | collective-permute-start | bytes 1572872 | tf_op jit(solution)/shard_map/ppermute | solution.py:177
  73.2 39.0 %collective-permute-start.4 = (bf16[256,1024]{1,0:T(8,128)(2,1)S(1)}, bf16[256,1024]{1,0:T(8,128)(2,1)S(1)}, u32[]{:S(2)}, u32[]{:S(2)}) collective-permute-start(bf16[256,1024]{1,0:T(8,128)(2,1)S(1)} %bitcast.24), channel_id=1, source_target_pairs={{0,192},{64,0},{128,64},{192,128},{1,193},{65,1},{129,65},{193,129... | collective-permute-start | bytes 1572872 | tf_op jit(solution)/shard_map/ppermute | solution.py:179
  76.5 47.0 %collective-permute-start.3 = (bf16[256,1024]{1,0:T(8,128)(2,1)S(1)}, bf16[256,1024]{1,0:T(8,128)(2,1)S(1)}, u32[]{:S(2)}, u32[]{:S(2)}) collective-permute-start(bf16[256,1024]{1,0:T(8,128)(2,1)S(1)} %bitcast.28), channel_id=1, source_target_pairs={{0,192},{64,0},{128,64},{192,128},{1,193},{65,1},{129,65},{193,129... | collective-permute-start | bytes 1572872 | tf_op jit(solution)/shard_map/ppermute | solution.py:178
  78.8 1.9 collective-permute-start
  80.7 42.9 %collective-permute-start.8 = (bf16[256,1024]{1,0:T(8,128)(2,1)S(1)}, bf16[256,1024]{1,0:T(8,128)(2,1)S(1)}, u32[]{:S(2)}, u32[]{:S(2)}) collective-permute-start(bf16[256,1024]{1,0:T(8,128)(2,1)S(1)} %bitcast.25), channel_id=1, source_target_pairs={{0,64},{64,128},{128,192},{192,0},{1,65},{65,129},{129,193},{193,1... | collective-permute-start | bytes 1572872 | tf_op jit(solution)/shard_map/ppermute | solution.py:180
  93.1 31.5 %collective-permute-start.6 = (bf16[256,1024]{1,0:T(8,128)(2,1)S(1)}, bf16[256,1024]{1,0:T(8,128)(2,1)}, u32[]{:S(2)}, u32[]{:S(2)}) collective-permute-start(bf16[256,1024]{1,0:T(8,128)(2,1)S(1)} %collective-permute-done.5.refs_6_), channel_id=1, source_target_pairs={{0,64},{64,128},{128,192},{192,0},{1,65},{65,129},{129,193},{193,1... | collective-permute-start | bytes 1572872 | tf_op jit(solution)/shard_map/ppermute | solution.py:181
  112.2 22.7 %collective-permute-start.7 = (bf16[256,1024]{1,0:T(8,128)(2,1)S(1)}, bf16[256,1024]{1,0:T(8,128)(2,1)}, u32[]{:S(2)}, u32[]{:S(2)}) collective-permute-start(bf16[256,1024]{1,0:T(8,128)(2,1)S(1)} %collective-permute-done.4.refs_3_), channel_id=1, source_target_pairs={{0,192},{64,0},{128,64},{192,128},{1,193},{65,1},{129,65},{193,129... | collective-permute-start | bytes 1572872 | tf_op jit(solution)/shard_map/ppermute | solution.py:182
  123.5 28.3 %collective-permute-start.1 = (bf16[512,256]{1,0:T(8,128)(2,1)S(1)}, bf16[512,256]{1,0:T(8,128)(2,1)}, u32[]{:S(2)}, u32[]{:S(2)}) collective-permute-start(bf16[512,256]{1,0:T(8,128)(2,1)S(1)} %maximum_select_fusion.2), channel_id=1, source_target_pairs={{0,2},{2,0},{1,3},{3,1},{4,6},{6,4},{5,7},{7,5},{8,10},{10,8},{9,1... | collective-permute-start | bytes 786440 | tf_op jit(solution)/shard_map/ppermute | solution.py:25
  123.6 29.6 %copy-start.5 = (s32[8]{0:T(128)S(1)}, s32[8]{0:T(128)}, u32[]{:S(2)}) copy-start(s32[8]{0:T(128)} %param.9) | copy-start | bytes 100
  144.1 31.7 %all-to-all-start = ((bf16[16,64,512]{2,1,0:T(8,128)(2,1)}), bf16[16,64,512]{2,1,0:T(8,128)(2,1)S(1)}, u32[]{:S(2)}, u32[]{:S(2)}) async-start(bf16[16,64,512]{2,1,0:T(8,128)(2,1)} %bitcast.17), calls=%async_computation | async-start | bytes 2097152 | tf_op jit(solution)/shard_map/all_to_all | solution.py:197
  153.1 21.1 %collective-permute-start.2 = (bf16[1024,256]{1,0:T(8,128)(2,1)S(1)}, bf16[1024,256]{1,0:T(8,128)(2,1)}, u32[]{:S(2)}, u32[]{:S(2)}) collective-permute-start(bf16[1024,256]{1,0:T(8,128)(2,1)S(1)} %maximum_select_fusion.1), channel_id=1, source_target_pairs={{0,4},{4,0},{1,5},{5,1},{2,6},{6,2},{3,7},{7,3},{8,12},{12,8},{9,1... | collective-permute-start | bytes 1572872 | tf_op jit(solution)/shard_map/ppermute | solution.py:25
  180.3 71.9 %copy-start.1 = (bf16[64,4096]{1,0:T(8,128)(2,1)S(1)}, bf16[64,4096]{1,0:T(8,128)(2,1)}, u32[]{:S(2)}) copy-start(bf16[64,4096]{1,0:T(8,128)(2,1)} %residual.1) | copy-start | bytes 1572868
  180.3 71.9 %copy-start.2 = (f32[4096]{0:T(1024)S(1)}, f32[4096]{0:T(1024)}, u32[]{:S(2)}) copy-start(f32[4096]{0:T(1024)} %param.13) | copy-start | bytes 49156
  180.3 19.9 %collective-permute-start.20 = (bf16[2,272,256]{2,1,0:T(8,128)(2,1)S(1)}, bf16[2,272,256]{2,1,0:T(8,128)(2,1)S(1)}, u32[]{:S(2)}, u32[]{:S(2)}) collective-permute-start(bf16[2,272,256]{2,1,0:T(8,128)(2,1)S(1)} %get-tuple-element.16), channel_id=1, source_target_pairs={{0,2},{2,0},{1,3},{3,1},{4,6},{6,4},{5,7},{7,5},{8,10},{10,8},{9,1... | collective-permute-start | bytes 835592 | tf_op jit(solution)/shard_map/ppermute | solution.py:25
  193.8 8.2 %collective-permute-start.21 = (bf16[2,272,256]{2,1,0:T(8,128)(2,1)S(1)}, bf16[2,272,256]{2,1,0:T(8,128)(2,1)S(1)}, u32[]{:S(2)}, u32[]{:S(2)}) collective-permute-start(bf16[2,272,256]{2,1,0:T(8,128)(2,1)S(1)} %get-tuple-element.17), channel_id=1, source_target_pairs={{0,4},{4,0},{1,5},{5,1},{2,6},{6,2},{3,7},{7,3},{8,12},{12,8},{9,1... | collective-permute-start | bytes 835592 | tf_op jit(solution)/shard_map/ppermute | solution.py:25
  194.3 12.0 %collective-permute-start.22 = (bf16[2,272,256]{2,1,0:T(8,128)(2,1)S(1)}, bf16[2,272,256]{2,1,0:T(8,128)(2,1)S(1)}, u32[]{:S(2)}, u32[]{:S(2)}) collective-permute-start(bf16[2,272,256]{2,1,0:T(8,128)(2,1)S(1)} %get-tuple-element.18), channel_id=1, source_target_pairs={{0,6},{2,4},{4,2},{6,0},{1,7},{3,5},{5,3},{7,1},{8,14},{10,12},{12... | collective-permute-start | bytes 835592 | tf_op jit(solution)/shard_map/ppermute | solution.py:204
  207.2 3.9 %collective-permute-start.23 = (bf16[256,256]{1,0:T(8,128)(2,1)S(1)}, bf16[256,256]{1,0:T(8,128)(2,1)S(1)}, u32[]{:S(2)}, u32[]{:S(2)}) collective-permute-start(bf16[256,256]{1,0:T(8,128)(2,1)S(1)} %get-tuple-element.20), channel_id=1, source_target_pairs={{0,1},{1,0},{2,3},{3,2},{4,5},{5,4},{6,7},{7,6},{8,9},{9,8},{10,11... | collective-permute-start | bytes 393224 | tf_op jit(solution)/shard_map/ppermute | solution.py:25
  211.0 2.2 copy-start
  215.0 25.9 %collective-permute-start.28 = (bf16[32,4096]{1,0:T(8,128)(2,1)S(1)}, bf16[32,4096]{1,0:T(8,128)(2,1)S(1)}, u32[]{:S(2)}, u32[]{:S(2)}) collective-permute-start(bf16[32,4096]{1,0:T(8,128)(2,1)S(1)} %get-tuple-element.27), channel_id=1, source_target_pairs={{0,192},{64,0},{128,64},{192,128},{1,193},{65,1},{129,65},{193,129... | collective-permute-start | bytes 786440 | tf_op jit(solution)/shard_map/ppermute | solution.py:210
  215.3 27.2 %collective-permute-start.24 = (bf16[32,4096]{1,0:T(8,128)(2,1)S(1)}, bf16[32,4096]{1,0:T(8,128)(2,1)S(1)}, u32[]{:S(2)}, u32[]{:S(2)}) collective-permute-start(bf16[32,4096]{1,0:T(8,128)(2,1)S(1)} %get-tuple-element.23), channel_id=1, source_target_pairs={{0,64},{64,128},{128,192},{192,0},{1,65},{65,129},{129,193},{193,1... | collective-permute-start | bytes 786440 | tf_op jit(solution)/shard_map/ppermute | solution.py:209
  217.5 26.1 %collective-permute-start.26 = (bf16[32,4096]{1,0:T(8,128)(2,1)S(1)}, bf16[32,4096]{1,0:T(8,128)(2,1)S(1)}, u32[]{:S(2)}, u32[]{:S(2)}) collective-permute-start(bf16[32,4096]{1,0:T(8,128)(2,1)S(1)} %get-tuple-element.24), channel_id=1, source_target_pairs={{0,64},{64,128},{128,192},{192,0},{1,65},{65,129},{129,193},{193,1... | collective-permute-start | bytes 786440 | tf_op jit(solution)/shard_map/ppermute | solution.py:211
  219.2 27.4 %collective-permute-start.27 = (bf16[32,4096]{1,0:T(8,128)(2,1)S(1)}, bf16[32,4096]{1,0:T(8,128)(2,1)S(1)}, u32[]{:S(2)}, u32[]{:S(2)}) collective-permute-start(bf16[32,4096]{1,0:T(8,128)(2,1)S(1)} %get-tuple-element.25), channel_id=1, source_target_pairs={{0,192},{64,0},{128,64},{192,128},{1,193},{65,1},{129,65},{193,129... | collective-permute-start | bytes 786440 | tf_op jit(solution)/shard_map/ppermute | solution.py:212
  241.0 11.2 %collective-permute-start.29 = (bf16[32,4096]{1,0:T(8,128)(2,1)S(1)}, bf16[32,4096]{1,0:T(8,128)(2,1)S(1)}, u32[]{:S(2)}, u32[]{:S(2)}) collective-permute-start(bf16[32,4096]{1,0:T(8,128)(2,1)S(1)} %add_convert_fusion), channel_id=1, source_target_pairs={{0,192},{64,0},{128,64},{192,128},{1,193},{65,1},{129,65},{193,129... | collective-permute-start | bytes 786440 | tf_op jit(solution)/shard_map/ppermute | solution.py:216
  242.6 9.6 %collective-permute-start.25 = (bf16[32,4096]{1,0:T(8,128)(2,1)S(1)}, bf16[32,4096]{1,0:T(8,128)(2,1)S(1)}, u32[]{:S(2)}, u32[]{:S(2)}) collective-permute-start(bf16[32,4096]{1,0:T(8,128)(2,1)S(1)} %add_convert_fusion.1), channel_id=1, source_target_pairs={{0,64},{64,128},{128,192},{192,0},{1,65},{65,129},{129,193},{193,1... | collective-permute-start | bytes 786440 | tf_op jit(solution)/shard_map/ppermute | solution.py:215

commit v2 on v1

--- a/solution.py
+++ b/solution.py
@@ -37,16 +37,19 @@
     return jnp.where(index == 0, a, b)
 
 
-def kernel_call(kernel, outs, where, *args):
+def kernel_call(kernel, outs, where, *args, far=(), scratch=()):
     spec = pl.BlockSpec(memory_space=pltpu.VMEM)
     args = [pltpu.with_memory_space_constraint(a, pltpu.VMEM) for a in args]
     return pl.pallas_call(
         kernel,
         out_shape=outs,
-        in_specs=[pl.BlockSpec(memory_space=pltpu.SMEM)] + [spec] * len(args),
+        in_specs=[pl.BlockSpec(memory_space=pltpu.SMEM)]
+        + [spec] * len(args)
+        + [pl.BlockSpec(memory_space=pl.ANY)] * len(far),
         out_specs=[spec] * len(outs),
+        scratch_shapes=scratch,
         compiler_params=pltpu.CompilerParams(vmem_limit_bytes=VMEM_LIMIT),
-    )(where, *args)
+    )(where, *args, *far)
 
 
 def project_kernel(where_ref, *refs):
@@ -118,8 +121,11 @@
     return kernel_call(merge_kernel, [jax.ShapeDtypeStruct((256, DH), BF)] * 2, where, *parts)
 
 
-def output_kernel(where_ref, mine, theirs, w_ref, own, fwd_a, fwd_b, bwd_a, bwd_b, far_a, far_b):
+def output_kernel(where_ref, mine, theirs, w_ref, own, fwd_a, fwd_b, bwd_a, bwd_b, far_a, far_b, buf, sem):
     zh, c = where_ref[0], where_ref[3]
+    copies = [pltpu.make_async_copy(w_ref.at[:, pl.ds(i * 512, 512)], buf.at[i], sem.at[i]) for i in range(8)]
+    for copy in copies:
+        copy.start()
 
     def by_distance(ref):
         return jnp.concatenate([ref[pl.ds(pl.multiple_of(lax.rem(zh + d, 4) * 64, 64), 64)] for d in range(4)], 0)
@@ -128,7 +134,8 @@
     heads = [pl.ds(pl.multiple_of(h * DH, DH), DH) for h in (c, 1 - c)]
     for i in range(8):
         cols = slice(i * 512, (i + 1) * 512)
-        acc = sum(jnp.dot(r, w_ref[h, cols], preferred_element_type=F32) for r, h in zip(rows, heads))
+        copies[i].wait()
+        acc = sum(jnp.dot(r, buf[i, h], preferred_element_type=F32) for r, h in zip(rows, heads))
         own[:, cols] = acc[:64]
         for at, out in ((64, fwd_a), (96, fwd_b), (128, far_a), (160, far_b), (192, bwd_a), (224, bwd_b)):
             out[:, cols] = acc[at : at + 32].astype(out.dtype)
@@ -137,7 +144,8 @@
 def output(where, mine, theirs, w):
     outs = [jax.ShapeDtypeStruct((64, 4096), F32)]
     outs += [jax.ShapeDtypeStruct((32, 4096), t) for t in (F32, BF, BF, F32, BF, BF)]
-    return kernel_call(output_kernel, outs, where, mine, theirs, w)
+    scratch = [pltpu.VMEM((8, 512, 512), BF), pltpu.SemaphoreType.DMA((8,))]
+    return kernel_call(output_kernel, outs, where, mine, theirs, far=(w,), scratch=scratch)
 
 
 def finish_kernel(where_ref, own, prev_a, prev_b, next_a, next_b, residual, gain, hidden, normed):

time: 255 us -> 257 us (level)
  no operation moved by 1% of the time
where the time goes in v2:
time: 257 us; the launch traced here: 256 us
  waiting for transfers between devices  163 us (63%)
  starting transfers between devices  57.1 us (22%)
  Pallas kernels  20.1 us (8%)
  local copies, waits for them, and re-layouts  9.69 us (4%)
  other arithmetic  5.02 us (2%)
    ppermute x9, waiting for transfers between devices, swap(): return lax.ppermute(a, axis, [(0, 1), (1, 0)])  35.4 us
    ppermute x9, starting transfers between devices, swap(): return lax.ppermute(a, axis, [(0, 1), (1, 0)])  24.7 us
    ppermute x1, waiting for transfers between devices, shards(): w_prev = lax.ppermute(w_near, Y, FWD)  22 us
    pallas_call x5, Pallas kernels, kernel_call(): pl.pallas_call(kernel, out_shape=outs, in_specs=[pl.BlockSpec(memory_spac...  20.1 us
    ppermute x1, waiting for transfers between devices, shards(): far_b = lax.ppermute(far_b, Z, BWD)  19.9 us
    ppermute x1, waiting for transfers between devices, shards(): next_b = lax.ppermute(mem_b, Z, BWD)  18.9 us
    ppermute x3, waiting for transfers between devices, beyond(): lax.ppermute(a, axis, [(i, (i + 4 - d) % 4) for i in range(4)])  13.4 us
    ppermute x1, waiting for transfers between devices, shards(): prev_a = lax.ppermute(mem_a, Z, FWD)  12.4 us
  transfers between devices with their start and end apart: 31, of which 21 were waited for; matrix products, arithmetic and copies ran while one was open for 4% of the time, Pallas kernels for 4%

profile of v2, /device:TPU:1, one launch (start us, length us, event | category | flops | bytes accessed | tf_op | source)
XLA Modules:
  0.0 255.9 jit_solution(3771268482389969621)
XLA Ops:
  1.5 3.3 %collective-permute-start.9 = (bf16[64,512]{1,0:T(8,128)(2,1)S(1)}, bf16[64,512]{1,0:T(8,128)(2,1)S(1)}, u32[]{:S(2)}, u32[]{:S(2)}) collective-permute-start(bf16[64,512]{1,0:T(8,128)(2,1)S(1)} %get-tuple-element.35), channel_id=1, source_target_pairs={{0,1},{1,0},{2,3},{3,2},{4,5},{5,4},{6,7},{7,6},{8,9},{9,8},{10,11... | collective-permute-start | bytes 196616 | tf_op jit(solution)/shard_map/ppermute | solution.py:25
  4.8 1.4 collective-permute-start.10
  6.3 3.4 %collective-permute-done.10 = bf16[64,512]{1,0:T(8,128)(2,1)S(1)} collective-permute-done((bf16[64,512]{1,0:T(8,128)(2,1)S(1)}, bf16[64,512]{1,0:T(8,128)(2,1)S(1)}, u32[]{:S(2)}, u32[]{:S(2)}) %collective-permute-start.10) | collective-permute-done | bytes 65568 | tf_op jit(solution)/shard_map/ppermute | solution.py:25
  12.4 4.4 %collective-permute-done.12 = bf16[256,512]{1,0:T(8,128)(2,1)S(1)} collective-permute-done((bf16[256,512]{1,0:T(8,128)(2,1)S(1)}, bf16[256,512]{1,0:T(8,128)(2,1)S(1)}, u32[]{:S(2)}, u32[]{:S(2)}) %collective-permute-start.12) | collective-permute-done | bytes 262176 | tf_op jit(solution)/shard_map/ppermute | solution.py:29
  16.8 1.3 collective-permute-done.13
  18.1 7.7 %collective-permute-done.14 = bf16[256,512]{1,0:T(8,128)(2,1)S(1)} collective-permute-done((bf16[256,512]{1,0:T(8,128)(2,1)S(1)}, bf16[256,512]{1,0:T(8,128)(2,1)S(1)}, u32[]{:S(2)}, u32[]{:S(2)}) %collective-permute-start.14) | collective-permute-done | bytes 262176 | tf_op jit(solution)/shard_map/ppermute | solution.py:29
  26.0 1.4 collective-permute-start.16
  27.4 1.5 collective-permute-start.15
  29.6 22.0 %collective-permute-done.16 = bf16[4,256,512]{2,1,0:T(8,128)(2,1)S(1)} collective-permute-done((bf16[4,256,512]{2,1,0:T(8,128)(2,1)S(1)}, bf16[4,256,512]{2,1,0:T(8,128)(2,1)S(1)}, u32[]{:S(2)}, u32[]{:S(2)}) %collective-permute-start.16) | collective-permute-done | bytes 1048608 | tf_op jit(solution)/shard_map/ppermute | solution.py:177
  51.8 2.7 %collective-permute-start.18 = (bf16[2,256,512]{2,1,0:T(8,128)(2,1)S(1)}, bf16[2,256,512]{2,1,0:T(8,128)(2,1)S(1)}, u32[]{:S(2)}, u32[]{:S(2)}) collective-permute-start(bf16[2,256,512]{2,1,0:T(8,128)(2,1)S(1)} %slice.37), channel_id=1, source_target_pairs={{0,12},{4,0},{8,4},{12,8},{1,13},{5,1},{9,5},{13,9},{2,14},{6,2},{... | collective-permute-start | bytes 1572872 | tf_op jit(solution)/shard_map/ppermute | solution.py:180
  56.0 1.1 constant_dynamic-update-slice_fusion.3
  57.1 8.1 %collective-permute-done.17 = bf16[2,256,512]{2,1,0:T(8,128)(2,1)S(1)} collective-permute-done((bf16[2,256,512]{2,1,0:T(8,128)(2,1)S(1)}, bf16[2,256,512]{2,1,0:T(8,128)(2,1)S(1)}, u32[]{:S(2)}, u32[]{:S(2)}) %collective-permute-start.17) | collective-permute-done | bytes 524320 | tf_op jit(solution)/shard_map/ppermute | solution.py:179
  66.8 1.1 constant_dynamic-update-slice_fusion
  67.9 2.1 collective-permute-start.19
  70.2 3.1 %collective-permute-start.5 = (bf16[256,1024]{1,0:T(8,128)(2,1)S(1)}, bf16[256,1024]{1,0:T(8,128)(2,1)S(1)}, u32[]{:S(2)}, u32[]{:S(2)}) collective-permute-start(bf16[256,1024]{1,0:T(8,128)(2,1)S(1)} %bitcast.27), channel_id=1, source_target_pairs={{0,64},{64,128},{128,192},{192,0},{1,65},{65,129},{129,193},{193,1... | collective-permute-start | bytes 1572872 | tf_op jit(solution)/shard_map/ppermute | solution.py:185
  73.2 3.3 %collective-permute-start.4 = (bf16[256,1024]{1,0:T(8,128)(2,1)S(1)}, bf16[256,1024]{1,0:T(8,128)(2,1)S(1)}, u32[]{:S(2)}, u32[]{:S(2)}) collective-permute-start(bf16[256,1024]{1,0:T(8,128)(2,1)S(1)} %bitcast.24), channel_id=1, source_target_pairs={{0,192},{64,0},{128,64},{192,128},{1,193},{65,1},{129,65},{193,129... | collective-permute-start | bytes 1572872 | tf_op jit(solution)/shard_map/ppermute | solution.py:187
  76.5 2.3 collective-permute-start.3
  79.7 1.0 collective-permute-done
  80.7 12.4 %collective-permute-done.5.refs_6_ = bf16[256,1024]{1,0:T(8,128)(2,1)S(1)} collective-permute-done((bf16[256,1024]{1,0:T(8,128)(2,1)S(1)}, bf16[256,1024]{1,0:T(8,128)(2,1)S(1)}, u32[]{:S(2)}, u32[]{:S(2)}) %collective-permute-start.5) | collective-permute-done | bytes 524320 | tf_op jit(solution)/shard_map/ppermute | solution.py:185
  93.3 18.9 %collective-permute-done.4.refs_3_ = bf16[256,1024]{1,0:T(8,128)(2,1)S(1)} collective-permute-done((bf16[256,1024]{1,0:T(8,128)(2,1)S(1)}, bf16[256,1024]{1,0:T(8,128)(2,1)S(1)}, u32[]{:S(2)}, u32[]{:S(2)}) %collective-permute-start.4) | collective-permute-done | bytes 524320 | tf_op jit(solution)/shard_map/ppermute | solution.py:187
  112.2 2.4 collective-permute-start.7
  114.7 8.8 %collective-permute-done.3.refs_2_ = bf16[256,1024]{1,0:T(8,128)(2,1)S(1)} collective-permute-done((bf16[256,1024]{1,0:T(8,128)(2,1)S(1)}, bf16[256,1024]{1,0:T(8,128)(2,1)S(1)}, u32[]{:S(2)}, u32[]{:S(2)}) %collective-permute-start.3) | collective-permute-done | bytes 524320 | tf_op jit(solution)/shard_map/ppermute | solution.py:186
  123.6 1.1 collective-permute-done.6.refs_4_
  124.7 10.2 %collective-permute-done.7.refs_5_ = bf16[256,1024]{1,0:T(8,128)(2,1)} collective-permute-done((bf16[256,1024]{1,0:T(8,128)(2,1)S(1)}, bf16[256,1024]{1,0:T(8,128)(2,1)}, u32[]{:S(2)}, u32[]{:S(2)}) %collective-permute-start.7) | collective-permute-done | bytes 524320 | tf_op jit(solution)/shard_map/ppermute | solution.py:190
  134.9 9.3 %shard_map.86 = bf16[8,2,64,512]{3,2,1,0:T(8,128)(2,1)} custom-call(s32[4]{0:T(128)S(1)} %pad_add_fusion.where_ref, bf16[256,1024]{1,0:T(8,128)(2,1)S(1)} %bitcast.29, bf16[256,1024]{1,0:T(8,128)(2,1)S(1)} %bitcast.26, bf16[256,1024]{1,0:T(8,128)(2,1)S(1)} %collective-permute-done.3.refs_2_, bf16[256,1024]{1,0:T(8,128)(2,1)S(1)} %collective-permute-done.4.refs_3_, ...), custom_call_target="tpu_custom_call" | custom-call | tf_op jit(solution)/shard_map/pallas_call | solution.py:43
  144.1 4.3 %all-to-all-start = ((bf16[16,64,512]{2,1,0:T(8,128)(2,1)}), bf16[16,64,512]{2,1,0:T(8,128)(2,1)S(1)}, u32[]{:S(2)}, u32[]{:S(2)}) async-start(bf16[16,64,512]{2,1,0:T(8,128)(2,1)} %bitcast.17), calls=%async_computation | async-start | bytes 2097152 | tf_op jit(solution)/shard_map/all_to_all | solution.py:205
  148.4 3.5 %collective-permute-done.1 = bf16[512,256]{1,0:T(8,128)(2,1)} collective-permute-done((bf16[512,256]{1,0:T(8,128)(2,1)S(1)}, bf16[512,256]{1,0:T(8,128)(2,1)}, u32[]{:S(2)}, u32[]{:S(2)}) %collective-permute-start.1) | collective-permute-done | bytes 262176 | tf_op jit(solution)/shard_map/ppermute | solution.py:25
  151.9 1.2 maximum_select_fusion.1
  154.6 19.7 %collective-permute-done.2 = bf16[1024,256]{1,0:T(8,128)(2,1)} collective-permute-done((bf16[1024,256]{1,0:T(8,128)(2,1)S(1)}, bf16[1024,256]{1,0:T(8,128)(2,1)}, u32[]{:S(2)}, u32[]{:S(2)}) %collective-permute-start.2) | collective-permute-done | bytes 524320 | tf_op jit(solution)/shard_map/ppermute | solution.py:25
  174.2 1.6 maximum_select_fusion.q_ref
  175.8 4.5 %shard_map.87 = (bf16[2,272,256]{2,1,0:T(8,128)(2,1)S(1)}, bf16[2,272,256]{2,1,0:T(8,128)(2,1)S(1)}, bf16[2,272,256]{2,1,0:T(8,128)(2,1)S(1)}, bf16[2,272,256]{2,1,0:T(8,128)(2,1)S(1)}) custom-call(s32[6]{0:T(128)S(1)} %stack.57.where_ref, bf16[2048,256]{1,0:T(8,128)(2,1)S(1)} %maximum_select_fusion.q_ref, bf16[1024,512]{1,0:T(8,128)(2,1)S(1)} %bitcast.23), custom_call_target="tpu_custom_call" | custom-call | tf_op jit(solution)/shard_map/pallas_call | solution.py:43
  180.3 13.5 %collective-permute-start.20 = (bf16[2,272,256]{2,1,0:T(8,128)(2,1)S(1)}, bf16[2,272,256]{2,1,0:T(8,128)(2,1)S(1)}, u32[]{:S(2)}, u32[]{:S(2)}) collective-permute-start(bf16[2,272,256]{2,1,0:T(8,128)(2,1)S(1)} %get-tuple-element.16), channel_id=1, source_target_pairs={{0,2},{2,0},{1,3},{3,1},{4,6},{6,4},{5,7},{7,5},{8,10},{10,8},{9,1... | collective-permute-start | bytes 835592 | tf_op jit(solution)/shard_map/ppermute | solution.py:25
  195.1 5.1 %collective-permute-done.20.b_ref = bf16[2,272,256]{2,1,0:T(8,128)(2,1)S(1)} collective-permute-done((bf16[2,272,256]{2,1,0:T(8,128)(2,1)S(1)}, bf16[2,272,256]{2,1,0:T(8,128)(2,1)S(1)}, u32[]{:S(2)}, u32[]{:S(2)}) %collective-permute-start.20) | collective-permute-done | bytes 278560 | tf_op jit(solution)/shard_map/ppermute | solution.py:25
  200.3 1.8 collective-permute-done.21.c_ref
  202.0 4.3 %collective-permute-done.22.d_ref = bf16[2,272,256]{2,1,0:T(8,128)(2,1)S(1)} collective-permute-done((bf16[2,272,256]{2,1,0:T(8,128)(2,1)S(1)}, bf16[2,272,256]{2,1,0:T(8,128)(2,1)S(1)}, u32[]{:S(2)}, u32[]{:S(2)}) %collective-permute-start.22) | collective-permute-done | bytes 278560 | tf_op jit(solution)/shard_map/ppermute | solution.py:212
  207.2 2.9 %collective-permute-start.23 = (bf16[256,256]{1,0:T(8,128)(2,1)S(1)}, bf16[256,256]{1,0:T(8,128)(2,1)S(1)}, u32[]{:S(2)}, u32[]{:S(2)}) collective-permute-start(bf16[256,256]{1,0:T(8,128)(2,1)S(1)} %get-tuple-element.20), channel_id=1, source_target_pairs={{0,1},{1,0},{2,3},{3,2},{4,5},{5,4},{6,7},{7,6},{8,9},{9,8},{10,11... | collective-permute-start | bytes 393224 | tf_op jit(solution)/shard_map/ppermute | solution.py:25
  210.1 1.0 collective-permute-done.23.theirs
  211.1 2.2 copy-done
  213.2 3.6 %shard_map.89 = (f32[64,4096]{1,0:T(8,128)S(1)}, f32[32,4096]{1,0:T(8,128)S(1)}, bf16[32,4096]{1,0:T(8,128)(2,1)S(1)}, bf16[32,4096]{1,0:T(8,128)(2,1)S(1)}, f32...) custom-call(s32[4]{0:T(128)S(1)} %pad_add_fusion.where_ref, ...), custom_call_target="tpu_custom_call" | custom-call | tf_op jit(solution)/shard_map/pallas_call | solution.py:43
  217.1 2.2 collective-permute-start.24
  219.3 1.7 collective-permute-start.26
  221.0 1.8 collective-permute-start.27
  222.9 19.9 %collective-permute-done.28 = bf16[32,4096]{1,0:T(8,128)(2,1)S(1)} collective-permute-done((bf16[32,4096]{1,0:T(8,128)(2,1)S(1)}, bf16[32,4096]{1,0:T(8,128)(2,1)S(1)}, u32[]{:S(2)}, u32[]{:S(2)}) %collective-permute-start.28) | collective-permute-done | bytes 262176 | tf_op jit(solution)/shard_map/ppermute | solution.py:218
  242.8 1.5 collective-permute-start.29
  244.4 1.0 collective-permute-start.25
  245.4 3.0 %collective-permute-done.27.next_a = bf16[32,4096]{1,0:T(8,128)(2,1)S(1)} collective-permute-done((bf16[32,4096]{1,0:T(8,128)(2,1)S(1)}, bf16[32,4096]{1,0:T(8,128)(2,1)S(1)}, u32[]{:S(2)}, u32[]{:S(2)}) %collective-permute-start.27) | collective-permute-done | bytes 262176 | tf_op jit(solution)/shard_map/ppermute | solution.py:220
  248.4 5.6 %collective-permute-done.29.next_b = bf16[32,4096]{1,0:T(8,128)(2,1)S(1)} collective-permute-done((bf16[32,4096]{1,0:T(8,128)(2,1)S(1)}, bf16[32,4096]{1,0:T(8,128)(2,1)S(1)}, u32[]{:S(2)}, u32[]{:S(2)}) %collective-permute-start.29) | collective-permute-done | bytes 262176 | tf_op jit(solution)/shard_map/ppermute | solution.py:224
  254.0 1.9 shard_map.90
  (56 shorter events, 13.1 us)
Async XLA Ops:
  1.5 4.7 %collective-permute-start.9 = (bf16[64,512]{1,0:T(8,128)(2,1)S(1)}, bf16[64,512]{1,0:T(8,128)(2,1)S(1)}, u32[]{:S(2)}, u32[]{:S(2)}) collective-permute-start(bf16[64,512]{1,0:T(8,128)(2,1)S(1)} %get-tuple-element.35), channel_id=1, source_target_pairs={{0,1},{1,0},{2,3},{3,2},{4,5},{5,4},{6,7},{7,6},{8,9},{9,8},{10,11... | collective-permute-start | bytes 196616 | tf_op jit(solution)/shard_map/ppermute | solution.py:25
  4.8 4.9 %collective-permute-start.11 = (bf16[64,512]{1,0:T(8,128)(2,1)S(1)}, bf16[64,512]{1,0:T(8,128)(2,1)S(1)}, u32[]{:S(2)}, u32[]{:S(2)}) collective-permute-start(bf16[64,512]{1,0:T(8,128)(2,1)S(1)} %get-tuple-element.35), channel_id=1, source_target_pairs={{0,3},{1,2},{2,1},{3,0},{4,7},{5,6},{6,5},{7,4},{8,11},{9,10},{10,... | collective-permute-start | bytes 196616 | tf_op jit(solution)/shard_map/ppermute | solution.py:173
  4.8 4.9 %collective-permute-start.10 = (bf16[64,512]{1,0:T(8,128)(2,1)S(1)}, bf16[64,512]{1,0:T(8,128)(2,1)S(1)}, u32[]{:S(2)}, u32[]{:S(2)}) collective-permute-start(bf16[64,512]{1,0:T(8,128)(2,1)S(1)} %get-tuple-element.34), channel_id=1, source_target_pairs={{0,2},{2,0},{1,3},{3,1},{4,6},{6,4},{5,7},{7,5},{8,10},{10,8},{9,1... | collective-permute-start | bytes 196616 | tf_op jit(solution)/shard_map/ppermute | solution.py:25
  9.8 7.0 %collective-permute-start.12 = (bf16[256,512]{1,0:T(8,128)(2,1)S(1)}, bf16[256,512]{1,0:T(8,128)(2,1)S(1)}, u32[]{:S(2)}, u32[]{:S(2)}) collective-permute-start(bf16[256,512]{1,0:T(8,128)(2,1)S(1)} %maximum_select_fusion.4), channel_id=1, source_target_pairs={{0,48},{16,0},{32,16},{48,32},{1,49},{17,1},{33,17},{49,33},{2,50}... | collective-permute-start | bytes 786440 | tf_op jit(solution)/shard_map/ppermute | solution.py:29
  10.5 7.6 %collective-permute-start.13 = (bf16[256,512]{1,0:T(8,128)(2,1)S(1)}, bf16[256,512]{1,0:T(8,128)(2,1)S(1)}, u32[]{:S(2)}, u32[]{:S(2)}) collective-permute-start(bf16[256,512]{1,0:T(8,128)(2,1)S(1)} %maximum_select_fusion.4), channel_id=1, source_target_pairs={{0,32},{16,48},{32,0},{48,16},{1,33},{17,49},{33,1},{49,17},{2,34}... | collective-permute-start | bytes 786440 | tf_op jit(solution)/shard_map/ppermute | solution.py:29
  11.0 14.8 %collective-permute-start.14 = (bf16[256,512]{1,0:T(8,128)(2,1)S(1)}, bf16[256,512]{1,0:T(8,128)(2,1)S(1)}, u32[]{:S(2)}, u32[]{:S(2)}) collective-permute-start(bf16[256,512]{1,0:T(8,128)(2,1)S(1)} %maximum_select_fusion.4), channel_id=1, source_target_pairs={{0,16},{16,32},{32,48},{48,0},{1,17},{17,33},{33,49},{49,1},{2,18}... | collective-permute-start | bytes 786440 | tf_op jit(solution)/shard_map/ppermute | solution.py:29
  26.0 25.6 %collective-permute-start.16 = (bf16[4,256,512]{2,1,0:T(8,128)(2,1)S(1)}, bf16[4,256,512]{2,1,0:T(8,128)(2,1)S(1)}, u32[]{:S(2)}, u32[]{:S(2)}) collective-permute-start(bf16[4,256,512]{2,1,0:T(8,128)(2,1)S(1)} %pad_maximum_fusion), channel_id=1, source_target_pairs={{0,4},{4,8},{8,12},{12,0},{1,5},{5,9},{9,13},{13,1},{2,6},{6,10},{... | collective-permute-start | bytes 3145736 | tf_op jit(solution)/shard_map/ppermute | solution.py:177
  27.4 24.4 %collective-permute-start.15 = (bf16[4,256,512]{2,1,0:T(8,128)(2,1)S(1)}, bf16[4,256,512]{2,1,0:T(8,128)(2,1)S(1)}, u32[]{:S(2)}, u32[]{:S(2)}) collective-permute-start(bf16[4,256,512]{2,1,0:T(8,128)(2,1)S(1)} %pad_maximum_fusion), channel_id=1, source_target_pairs={{0,12},{4,0},{8,4},{12,8},{1,13},{5,1},{9,5},{13,9},{2,14},{6,2},{... | collective-permute-start | bytes 3145736 | tf_op jit(solution)/shard_map/ppermute | solution.py:178
  51.7 18.4 %copy-start.3 = (bf16[8,64,1024]{2,1,0:T(8,128)(2,1)S(1)}, bf16[8,64,1024]{2,1,0:T(8,128)(2,1)}, u32[]{:S(2)}) copy-start(bf16[8,64,1024]{2,1,0:T(8,128)(2,1)} %param.7) | copy-start | bytes 3145732
  51.7 13.5 %collective-permute-start.17 = (bf16[2,256,512]{2,1,0:T(8,128)(2,1)S(1)}, bf16[2,256,512]{2,1,0:T(8,128)(2,1)S(1)}, u32[]{:S(2)}, u32[]{:S(2)}) collective-permute-start(bf16[2,256,512]{2,1,0:T(8,128)(2,1)S(1)} %slice.36), channel_id=1, source_target_pairs={{0,4},{4,8},{8,12},{12,0},{1,5},{5,9},{9,13},{13,1},{2,6},{6,10},{... | collective-permute-start | bytes 1572872 | tf_op jit(solution)/shard_map/ppermute | solution.py:179
  51.8 14.2 %collective-permute-start.18 = (bf16[2,256,512]{2,1,0:T(8,128)(2,1)S(1)}, bf16[2,256,512]{2,1,0:T(8,128)(2,1)S(1)}, u32[]{:S(2)}, u32[]{:S(2)}) collective-permute-start(bf16[2,256,512]{2,1,0:T(8,128)(2,1)S(1)} %slice.37), channel_id=1, source_target_pairs={{0,12},{4,0},{8,4},{12,8},{1,13},{5,1},{9,5},{13,9},{2,14},{6,2},{... | collective-permute-start | bytes 1572872 | tf_op jit(solution)/shard_map/ppermute | solution.py:180
  56.0 22.8 %copy-start.4 = (bf16[256,512]{1,0:T(8,128)(2,1)S(1)}, bf16[256,512]{1,0:T(8,128)(2,1)}, u32[]{:S(2)}) copy-start(bf16[256,512]{1,0:T(8,128)(2,1)} %param.10) | copy-start | bytes 786436
  67.9 66.9 %collective-permute-start.19 = (bf16[4,4,256,512]{3,2,1,0:T(8,128)(2,1)}, bf16[4,4,256,512]{3,2,1,0:T(8,128)(2,1)}, u32[]{:S(2)}, u32[]{:S(2)}) collective-permute-start(bf16[4,4,256,512]{3,2,1,0:T(8,128)(2,1)} %bitcast.16.refs_8_), channel_id=1, source_target_pairs={{0,1},{1,0},{2,3},{3,2},{4,5},{5,4},{6,7},{7,6},{8,9},{9,8},{10,11... | collective-permute-start | bytes 12582920 | tf_op jit(solution)/shard_map/ppermute | solution.py:25
  70.2 23.0 %collective-permute-start.5 = (bf16[256,1024]{1,0:T(8,128)(2,1)S(1)}, bf16[256,1024]{1,0:T(8,128)(2,1)S(1)}, u32[]{:S(2)}, u32[]{:S(2)}) collective-permute-start(bf16[256,1024]{1,0:T(8,128)(2,1)S(1)} %bitcast.27), channel_id=1, source_target_pairs={{0,64},{64,128},{128,192},{192,0},{1,65},{65,129},{129,193},{193,1... | collective-permute-start | bytes 1572872 | tf_op jit(solution)/shard_map/ppermute | solution.py:185
  73.2 39.0 %collective-permute-start.4 = (bf16[256,1024]{1,0:T(8,128)(2,1)S(1)}, bf16[256,1024]{1,0:T(8,128)(2,1)S(1)}, u32[]{:S(2)}, u32[]{:S(2)}) collective-permute-start(bf16[256,1024]{1,0:T(8,128)(2,1)S(1)} %bitcast.24), channel_id=1, source_target_pairs={{0,192},{64,0},{128,64},{192,128},{1,193},{65,1},{129,65},{193,129... | collective-permute-start | bytes 1572872 | tf_op jit(solution)/shard_map/ppermute | solution.py:187
  76.5 47.0 %collective-permute-start.3 = (bf16[256,1024]{1,0:T(8,128)(2,1)S(1)}, bf16[256,1024]{1,0:T(8,128)(2,1)S(1)}, u32[]{:S(2)}, u32[]{:S(2)}) collective-permute-start(bf16[256,1024]{1,0:T(8,128)(2,1)S(1)} %bitcast.28), channel_id=1, source_target_pairs={{0,192},{64,0},{128,64},{192,128},{1,193},{65,1},{129,65},{193,129... | collective-permute-start | bytes 1572872 | tf_op jit(solution)/shard_map/ppermute | solution.py:186
  78.8 1.9 collective-permute-start
  80.7 42.9 %collective-permute-start.8 = (bf16[256,1024]{1,0:T(8,128)(2,1)S(1)}, bf16[256,1024]{1,0:T(8,128)(2,1)S(1)}, u32[]{:S(2)}, u32[]{:S(2)}) collective-permute-start(bf16[256,1024]{1,0:T(8,128)(2,1)S(1)} %bitcast.25), channel_id=1, source_target_pairs={{0,64},{64,128},{128,192},{192,0},{1,65},{65,129},{129,193},{193,1... | collective-permute-start | bytes 1572872 | tf_op jit(solution)/shard_map/ppermute | solution.py:188
  93.1 31.5 %collective-permute-start.6 = (bf16[256,1024]{1,0:T(8,128)(2,1)S(1)}, bf16[256,1024]{1,0:T(8,128)(2,1)}, u32[]{:S(2)}, u32[]{:S(2)}) collective-permute-start(bf16[256,1024]{1,0:T(8,128)(2,1)S(1)} %collective-permute-done.5.refs_6_), channel_id=1, source_target_pairs={{0,64},{64,128},{128,192},{192,0},{1,65},{65,129},{129,193},{193,1... | collective-permute-start | bytes 1572872 | tf_op jit(solution)/shard_map/ppermute | solution.py:189
  112.2 22.7 %collective-permute-start.7 = (bf16[256,1024]{1,0:T(8,128)(2,1)S(1)}, bf16[256,1024]{1,0:T(8,128)(2,1)}, u32[]{:S(2)}, u32[]{:S(2)}) collective-permute-start(bf16[256,1024]{1,0:T(8,128)(2,1)S(1)} %collective-permute-done.4.refs_3_), channel_id=1, source_target_pairs={{0,192},{64,0},{128,64},{192,128},{1,193},{65,1},{129,65},{193,129... | collective-permute-start | bytes 1572872 | tf_op jit(solution)/shard_map/ppermute | solution.py:190
  123.5 28.3 %collective-permute-start.1 = (bf16[512,256]{1,0:T(8,128)(2,1)S(1)}, bf16[512,256]{1,0:T(8,128)(2,1)}, u32[]{:S(2)}, u32[]{:S(2)}) collective-permute-start(bf16[512,256]{1,0:T(8,128)(2,1)S(1)} %maximum_select_fusion.2), channel_id=1, source_target_pairs={{0,2},{2,0},{1,3},{3,1},{4,6},{6,4},{5,7},{7,5},{8,10},{10,8},{9,1... | collective-permute-start | bytes 786440 | tf_op jit(solution)/shard_map/ppermute | solution.py:25
  123.6 29.6 %copy-start.5 = (s32[8]{0:T(128)S(1)}, s32[8]{0:T(128)}, u32[]{:S(2)}) copy-start(s32[8]{0:T(128)} %param.9) | copy-start | bytes 100
  144.1 31.7 %all-to-all-start = ((bf16[16,64,512]{2,1,0:T(8,128)(2,1)}), bf16[16,64,512]{2,1,0:T(8,128)(2,1)S(1)}, u32[]{:S(2)}, u32[]{:S(2)}) async-start(bf16[16,64,512]{2,1,0:T(8,128)(2,1)} %bitcast.17), calls=%async_computation | async-start | bytes 2097152 | tf_op jit(solution)/shard_map/all_to_all | solution.py:205
  153.1 21.1 %collective-permute-start.2 = (bf16[1024,256]{1,0:T(8,128)(2,1)S(1)}, bf16[1024,256]{1,0:T(8,128)(2,1)}, u32[]{:S(2)}, u32[]{:S(2)}) collective-permute-start(bf16[1024,256]{1,0:T(8,128)(2,1)S(1)} %maximum_select_fusion.1), channel_id=1, source_target_pairs={{0,4},{4,0},{1,5},{5,1},{2,6},{6,2},{3,7},{7,3},{8,12},{12,8},{9,1... | collective-permute-start | bytes 1572872 | tf_op jit(solution)/shard_map/ppermute | solution.py:25
  180.3 73.7 %copy-start.1 = (bf16[64,4096]{1,0:T(8,128)(2,1)S(1)}, bf16[64,4096]{1,0:T(8,128)(2,1)}, u32[]{:S(2)}) copy-start(bf16[64,4096]{1,0:T(8,128)(2,1)} %residual.1) | copy-start | bytes 1572868
  180.3 73.7 %copy-start.2 = (f32[4096]{0:T(1024)S(1)}, f32[4096]{0:T(1024)}, u32[]{:S(2)}) copy-start(f32[4096]{0:T(1024)} %param.13) | copy-start | bytes 49156
  180.3 19.9 %collective-permute-start.20 = (bf16[2,272,256]{2,1,0:T(8,128)(2,1)S(1)}, bf16[2,272,256]{2,1,0:T(8,128)(2,1)S(1)}, u32[]{:S(2)}, u32[]{:S(2)}) collective-permute-start(bf16[2,272,256]{2,1,0:T(8,128)(2,1)S(1)} %get-tuple-element.16), channel_id=1, source_target_pairs={{0,2},{2,0},{1,3},{3,1},{4,6},{6,4},{5,7},{7,5},{8,10},{10,8},{9,1... | collective-permute-start | bytes 835592 | tf_op jit(solution)/shard_map/ppermute | solution.py:25
  193.8 8.2 %collective-permute-start.21 = (bf16[2,272,256]{2,1,0:T(8,128)(2,1)S(1)}, bf16[2,272,256]{2,1,0:T(8,128)(2,1)S(1)}, u32[]{:S(2)}, u32[]{:S(2)}) collective-permute-start(bf16[2,272,256]{2,1,0:T(8,128)(2,1)S(1)} %get-tuple-element.17), channel_id=1, source_target_pairs={{0,4},{4,0},{1,5},{5,1},{2,6},{6,2},{3,7},{7,3},{8,12},{12,8},{9,1... | collective-permute-start | bytes 835592 | tf_op jit(solution)/shard_map/ppermute | solution.py:25
  194.3 12.0 %collective-permute-start.22 = (bf16[2,272,256]{2,1,0:T(8,128)(2,1)S(1)}, bf16[2,272,256]{2,1,0:T(8,128)(2,1)S(1)}, u32[]{:S(2)}, u32[]{:S(2)}) collective-permute-start(bf16[2,272,256]{2,1,0:T(8,128)(2,1)S(1)} %get-tuple-element.18), channel_id=1, source_target_pairs={{0,6},{2,4},{4,2},{6,0},{1,7},{3,5},{5,3},{7,1},{8,14},{10,12},{12... | collective-permute-start | bytes 835592 | tf_op jit(solution)/shard_map/ppermute | solution.py:212
  207.2 3.9 %collective-permute-start.23 = (bf16[256,256]{1,0:T(8,128)(2,1)S(1)}, bf16[256,256]{1,0:T(8,128)(2,1)S(1)}, u32[]{:S(2)}, u32[]{:S(2)}) collective-permute-start(bf16[256,256]{1,0:T(8,128)(2,1)S(1)} %get-tuple-element.20), channel_id=1, source_target_pairs={{0,1},{1,0},{2,3},{3,2},{4,5},{5,4},{6,7},{7,6},{8,9},{9,8},{10,11... | collective-permute-start | bytes 393224 | tf_op jit(solution)/shard_map/ppermute | solution.py:25
  211.0 2.2 copy-start
  216.8 25.9 %collective-permute-start.28 = (bf16[32,4096]{1,0:T(8,128)(2,1)S(1)}, bf16[32,4096]{1,0:T(8,128)(2,1)S(1)}, u32[]{:S(2)}, u32[]{:S(2)}) collective-permute-start(bf16[32,4096]{1,0:T(8,128)(2,1)S(1)} %get-tuple-element.27), channel_id=1, source_target_pairs={{0,192},{64,0},{128,64},{192,128},{1,193},{65,1},{129,65},{193,129... | collective-permute-start | bytes 786440 | tf_op jit(solution)/shard_map/ppermute | solution.py:218
  217.1 27.2 %collective-permute-start.24 = (bf16[32,4096]{1,0:T(8,128)(2,1)S(1)}, bf16[32,4096]{1,0:T(8,128)(2,1)S(1)}, u32[]{:S(2)}, u32[]{:S(2)}) collective-permute-start(bf16[32,4096]{1,0:T(8,128)(2,1)S(1)} %get-tuple-element.23), channel_id=1, source_target_pairs={{0,64},{64,128},{128,192},{192,0},{1,65},{65,129},{129,193},{193,1... | collective-permute-start | bytes 786440 | tf_op jit(solution)/shard_map/ppermute | solution.py:217
  219.3 26.1 %collective-permute-start.26 = (bf16[32,4096]{1,0:T(8,128)(2,1)S(1)}, bf16[32,4096]{1,0:T(8,128)(2,1)S(1)}, u32[]{:S(2)}, u32[]{:S(2)}) collective-permute-start(bf16[32,4096]{1,0:T(8,128)(2,1)S(1)} %get-tuple-element.24), channel_id=1, source_target_pairs={{0,64},{64,128},{128,192},{192,0},{1,65},{65,129},{129,193},{193,1... | collective-permute-start | bytes 786440 | tf_op jit(solution)/shard_map/ppermute | solution.py:219
  221.0 27.4 %collective-permute-start.27 = (bf16[32,4096]{1,0:T(8,128)(2,1)S(1)}, bf16[32,4096]{1,0:T(8,128)(2,1)S(1)}, u32[]{:S(2)}, u32[]{:S(2)}) collective-permute-start(bf16[32,4096]{1,0:T(8,128)(2,1)S(1)} %get-tuple-element.25), channel_id=1, source_target_pairs={{0,192},{64,0},{128,64},{192,128},{1,193},{65,1},{129,65},{193,129... | collective-permute-start | bytes 786440 | tf_op jit(solution)/shard_map/ppermute | solution.py:220
  242.8 11.2 %collective-permute-start.29 = (bf16[32,4096]{1,0:T(8,128)(2,1)S(1)}, bf16[32,4096]{1,0:T(8,128)(2,1)S(1)}, u32[]{:S(2)}, u32[]{:S(2)}) collective-permute-start(bf16[32,4096]{1,0:T(8,128)(2,1)S(1)} %add_convert_fusion), channel_id=1, source_target_pairs={{0,192},{64,0},{128,64},{192,128},{1,193},{65,1},{129,65},{193,129... | collective-permute-start | bytes 786440 | tf_op jit(solution)/shard_map/ppermute | solution.py:224
  244.4 9.6 %collective-permute-start.25 = (bf16[32,4096]{1,0:T(8,128)(2,1)S(1)}, bf16[32,4096]{1,0:T(8,128)(2,1)S(1)}, u32[]{:S(2)}, u32[]{:S(2)}) collective-permute-start(bf16[32,4096]{1,0:T(8,128)(2,1)S(1)} %add_convert_fusion.1), channel_id=1, source_target_pairs={{0,64},{64,128},{128,192},{192,0},{1,65},{65,129},{129,193},{193,1... | collective-permute-start | bytes 786440 | tf_op jit(solution)/shard_map/ppermute | solution.py:223

commit v3 on v1

--- a/solution.py
+++ b/solution.py
@@ -49,31 +49,40 @@
     )(where, *args)
 
 
-def project_kernel(where_ref, *refs):
-    pieces, (w_mine, w_theirs, out_ref) = refs[:8], refs[8:]
+def project_kernel(where_ref, own, nxt, opp_a, opp_b, prev, w_mine, w_theirs, out_ref):
     zh, x, y, c = where_ref[0], where_ref[1], where_ref[2], where_ref[3]
-    acc = [jnp.zeros((512, 2 * DH), F32)] * 2
+    acc = [jnp.zeros((own.shape[0], 2 * DH), F32)] * 2
     near = [lax.rem(i + 4 - y, 4) for i in range(4)]
     for dz in range(4):
         dx = lax.rem(zh + dz + 4 - x, 4)
-        rows = jnp.concatenate([pieces[2 * dz][...], pieces[2 * dz + 1][...]], 0)
+        if dz == 2:
+            rows = jnp.concatenate([opp_a[...], opp_b[...]], 0)
+        else:
+            rows = (own, nxt, None, prev)[dz][...]
         for j, w in enumerate((w_mine, w_theirs)):
             block = jnp.concatenate([w[dy, dx] for dy in near], 0)
             acc[j] = acc[j] + jnp.dot(rows, block, preferred_element_type=F32)
-    out_ref[:, c] = acc[0].astype(BF).reshape(8, 64, 2 * DH)
-    out_ref[:, 1 - c] = acc[1].astype(BF).reshape(8, 64, 2 * DH)
+    shape = (out_ref.shape[0],) + out_ref.shape[2:]
+    out_ref[:, c] = acc[0].astype(BF).reshape(shape)
+    out_ref[:, 1 - c] = acc[1].astype(BF).reshape(shape)
 
 
 def project(where, pieces, weights):
-    out = jax.ShapeDtypeStruct((8, 2, 64, 2 * DH), BF)
+    out = jax.ShapeDtypeStruct((8, 2, pieces[0].shape[0] // 8, 2 * DH), BF)
     return kernel_call(project_kernel, [out], where, *pieces, *weights)[0]
 
 
-def attend_kernel(where_ref, q_ref, kv_ref, *outs):
+def attend_kernel(chunk, last, where_ref, q_ref, kv_ref, *refs):
     length, base = where_ref[0], where_ref[1]
     rows = kv_ref.shape[0]
+    per = rows // 16
+    if last:
+        acc_in, stats_in, outs = refs[0], refs[1], refs[2:]
+    else:
+        acc_out, stats_out = refs
     row = lax.broadcasted_iota(jnp.int32, (rows, 128), 0)
-    position = (row >> 7) * 512 + base + (row & 127)
+    shift = per.bit_length() - 1
+    position = (row >> (shift + 1)) * 512 + base + ((row >> shift) & 1) * 64 + chunk * per + (row & (per - 1))
     bias = jnp.where(position < length, 0.0, -1e30)
     bias = jnp.concatenate([bias, bias], axis=1)
     keys = kv_ref[:, :DH]
@@ -83,9 +92,19 @@
         q = q_ref[pl.ds(pl.multiple_of(group * 256, 256), 256)]
         s = lax.dot_general(keys, q, (((1,), (1,)), ((), ())), preferred_element_type=F32) + bias
         high = jnp.max(s, axis=0, keepdims=True)
+        if last:
+            before = stats_in[i, 0:1]
+            high = jnp.maximum(high, before)
         p = jnp.exp2((s - high) * EXP_SCALE)
         total = jnp.sum(p, axis=0, keepdims=True)
         acc = jnp.dot(values, p.astype(BF), preferred_element_type=F32)
+        if not last:
+            acc_out[i] = acc
+            stats_out[i] = jnp.concatenate([high, total, jnp.zeros((6, 256), F32)], 0)
+            continue
+        keep = jnp.exp2((before - high) * EXP_SCALE)
+        total = total + stats_in[i, 1:2] * keep
+        acc = acc + acc_in[i] * keep
         lse = high * EXP_SCALE + jnp.log2(total)
         first = lse.astype(BF).astype(F32)
         second = (lse - first).astype(BF).astype(F32)
@@ -94,8 +113,14 @@
         outs[i // 2][i % 2, DH:] = stats.astype(BF)
 
 
-def attend(where, q, kv):
-    return kernel_call(attend_kernel, [jax.ShapeDtypeStruct((2, DH + 16, 256), BF)] * 4, where, q, kv)
+def attend(where, q, kv, chunk, before=None):
+    last = before is not None
+    if last:
+        outs = [jax.ShapeDtypeStruct((2, DH + 16, 256), BF)] * 4
+    else:
+        outs = [jax.ShapeDtypeStruct((8, DH, 256), F32), jax.ShapeDtypeStruct((8, 8, 256), F32)]
+    kernel = functools.partial(attend_kernel, chunk, last)
+    return kernel_call(kernel, outs, where, q, kv, *(before or ()))
 
 
 def merge_kernel(where_ref, a_ref, b_ref, c_ref, d_ref, *outs):
@@ -173,14 +198,16 @@
     w_mine = jnp.concatenate([w_near, w_next, w_far_a, w_far_b, w_prev], 0).reshape((4,) + w_near.shape)
     w_theirs = swap(w_mine, "c")
 
-    mem_a, mem_b = memory[:4].reshape(256, 1024), memory[4:].reshape(256, 1024)
-    prev_a = lax.ppermute(mem_a, Z, FWD)
-    next_a = lax.ppermute(mem_a, Z, BWD)
-    next_b = lax.ppermute(mem_b, Z, BWD)
-    prev_b = lax.ppermute(mem_b, Z, FWD)
-    far_a = lax.ppermute(prev_a, Z, FWD)
-    far_b = lax.ppermute(next_b, Z, BWD)
-    pieces = (mem_a, mem_b, next_a, next_b, far_a, far_b, prev_a, prev_b)
+    step = memory.shape[1] // 2
+    half = 4 * step
+    chunks = []
+    for j in range(2):
+        own = memory[:, j * step : (j + 1) * step].reshape(8 * step, 1024)
+        prev = lax.ppermute(own, Z, FWD)
+        nxt = lax.ppermute(own, Z, BWD)
+        opp_a = lax.ppermute(prev[:half], Z, FWD)
+        opp_b = lax.ppermute(nxt[half:], Z, BWD)
+        chunks.append((own, nxt, opp_a, opp_b, prev))
 
     other = pick(queries[:, DH:], queries[:, :DH], c)
     other = swap(other, "c")
@@ -193,9 +220,12 @@
     length = lax.dynamic_index_in_dim(mem_lengths, x * 2 + yh, 0, keepdims=False)
     here = yl * 2 + zl
     here = jnp.stack([length, yl * 256 + zl * 128, here, here ^ 1, here ^ 2, here ^ 3]).astype(jnp.int32)
-    both = project(where, pieces, (w_mine, w_theirs))
-    both = lax.all_to_all(both.reshape(16, 64, 512), (X, "yh", "c"), 0, 0, tiled=True)
-    own, to_zl, to_yl, to_both = attend(here, q, both.reshape(1024, 512))
+    state = None
+    for j, pieces in enumerate(chunks):
+        both = project(where, pieces, (w_mine, w_theirs))
+        both = lax.all_to_all(both.reshape(16, step, 512), (X, "yh", "c"), 0, 0, tiled=True)
+        state = attend(here, q, both.reshape(16 * step, 512), j, state)
+    own, to_zl, to_yl, to_both = state
 
     parts = (
         own,

time: 255 us -> 261 us (1.024)
  waiting for transfers between devices: 163 us -> 156 us
  starting transfers between devices: 57.1 us -> 64.1 us
  Pallas kernels: 18.3 us -> 24 us
    ppermute x9, waiting for transfers between devices: 35.4 us -> 15.8 us  [swap(): return lax.ppermute(a, axis, [(0, 1), (1, 0)])]
    ppermute x9, starting transfers between devices: 24.7 us -> 13.5 us  [swap(): return lax.ppermute(a, axis, [(0, 1), (1, 0)])]
    ppermute x6 -> x8, waiting for transfers between devices: 51.4 us -> 62.4 us  [the longest x2 28.2 us: shards(): opp_b = lax.ppermute(nxt[half:], Z, BWD)]
    ppermute x6 -> x8, starting transfers between devices: 11.2 us -> 21.5 us  [the longest x2 10.1 us: shards(): opp_a = lax.ppermute(prev[:half], Z, FWD)]
    all_to_all x1 -> x2, starting transfers between devices: 4.29 us -> 11.8 us  [shards(): lax.all_to_all(both.reshape(16, step, 512), (X, 'yh', 'c'), 0, 0, tiled=T...]
    pallas_call x5 -> x7, Pallas kernels: 18.3 us -> 24 us  [kernel_call(): pl.pallas_call(kernel, out_shape=outs, in_specs=[pl.BlockSpec(memory_spac...]
    all_to_all x1 -> x2, waiting for transfers between devices: 0.01 us -> 4.75 us  [shards(): lax.all_to_all(both.reshape(16, step, 512), (X, 'yh', 'c'), 0, 0, tiled=T...]
    ppermute x1, waiting for transfers between devices: 4.27 us -> 0.01 us  [shards(): lax.ppermute(to_both, ('yl', 'zl'), [(i, 3 - i) for i in range(4)])]
  transfers between devices with their start and end apart: 31 -> 34, of which waited for: 21 -> 19; matrix products, arithmetic and copies ran while one was open for 4% -> 4% of each run, Pallas kernels for 4% -> 6%
where the time goes in v3:
time: 261 us; the launch traced here: 260 us
  waiting for transfers between devices  156 us (60%)
  starting transfers between devices  64.1 us (25%)
  Pallas kernels  24 us (9%)
  local copies, waits for them, and re-layouts  9.31 us (4%)
  other arithmetic  5.76 us (2%)
    ppermute x2, waiting for transfers between devices, shards(): opp_b = lax.ppermute(nxt[half:], Z, BWD)  28.2 us
    pallas_call x7, Pallas kernels, kernel_call(): pl.pallas_call(kernel, out_shape=outs, in_specs=[pl.BlockSpec(memory_spac...  24 us
    ppermute x1, waiting for transfers between devices, shards(): w_prev = lax.ppermute(w_near, Y, FWD)  22 us
    ppermute x1, waiting for transfers between devices, shards(): far_b = lax.ppermute(far_b, Z, BWD)  20 us
    ppermute x2, waiting for transfers between devices, shards(): opp_a = lax.ppermute(prev[:half], Z, FWD)  17.5 us
    ppermute x2, waiting for transfers between devices, shards(): prev = lax.ppermute(own, Z, FWD)  16.6 us
    ppermute x9, waiting for transfers between devices, swap(): return lax.ppermute(a, axis, [(0, 1), (1, 0)])  15.8 us
    ppermute x9, starting transfers between devices, swap(): return lax.ppermute(a, axis, [(0, 1), (1, 0)])  13.5 us
  transfers between devices with their start and end apart: 34, of which 19 were waited for; matrix products, arithmetic and copies ran while one was open for 4% of the time, Pallas kernels for 6%

profile of v3, /device:TPU:1, one launch (start us, length us, event | category | flops | bytes accessed | tf_op | source)
XLA Modules:
  0.0 259.6 jit_solution(17863184526663366257)
XLA Ops:
  1.5 3.3 %collective-permute-start.7 = (bf16[64,512]{1,0:T(8,128)(2,1)S(1)}, bf16[64,512]{1,0:T(8,128)(2,1)S(1)}, u32[]{:S(2)}, u32[]{:S(2)}) collective-permute-start(bf16[64,512]{1,0:T(8,128)(2,1)S(1)} %get-tuple-element.39), channel_id=1, source_target_pairs={{0,1},{1,0},{2,3},{3,2},{4,5},{5,4},{6,7},{7,6},{8,9},{9,8},{10,11... | collective-permute-start | bytes 196616 | tf_op jit(solution)/shard_map/ppermute | solution.py:25
  4.8 1.4 collective-permute-start.8
  6.3 3.4 %collective-permute-done.8 = bf16[64,512]{1,0:T(8,128)(2,1)S(1)} collective-permute-done((bf16[64,512]{1,0:T(8,128)(2,1)S(1)}, bf16[64,512]{1,0:T(8,128)(2,1)S(1)}, u32[]{:S(2)}, u32[]{:S(2)}) %collective-permute-start.8) | collective-permute-done | bytes 65568 | tf_op jit(solution)/shard_map/ppermute | solution.py:25
  12.4 4.4 %collective-permute-done.10 = bf16[256,512]{1,0:T(8,128)(2,1)S(1)} collective-permute-done((bf16[256,512]{1,0:T(8,128)(2,1)S(1)}, bf16[256,512]{1,0:T(8,128)(2,1)S(1)}, u32[]{:S(2)}, u32[]{:S(2)}) %collective-permute-start.10) | collective-permute-done | bytes 262176 | tf_op jit(solution)/shard_map/ppermute | solution.py:29
  16.8 1.3 collective-permute-done.11
  18.1 7.7 %collective-permute-done.12 = bf16[256,512]{1,0:T(8,128)(2,1)S(1)} collective-permute-done((bf16[256,512]{1,0:T(8,128)(2,1)S(1)}, bf16[256,512]{1,0:T(8,128)(2,1)S(1)}, u32[]{:S(2)}, u32[]{:S(2)}) %collective-permute-start.12) | collective-permute-done | bytes 262176 | tf_op jit(solution)/shard_map/ppermute | solution.py:29
  26.0 1.4 collective-permute-start.14
  27.4 1.5 collective-permute-start.13
  29.6 22.0 %collective-permute-done.14 = bf16[4,256,512]{2,1,0:T(8,128)(2,1)S(1)} collective-permute-done((bf16[4,256,512]{2,1,0:T(8,128)(2,1)S(1)}, bf16[4,256,512]{2,1,0:T(8,128)(2,1)S(1)}, u32[]{:S(2)}, u32[]{:S(2)}) %collective-permute-start.14) | collective-permute-done | bytes 1048608 | tf_op jit(solution)/shard_map/ppermute | solution.py:194
  51.8 2.7 %collective-permute-start.16 = (bf16[2,256,512]{2,1,0:T(8,128)(2,1)S(1)}, bf16[2,256,512]{2,1,0:T(8,128)(2,1)S(1)}, u32[]{:S(2)}, u32[]{:S(2)}) collective-permute-start(bf16[2,256,512]{2,1,0:T(8,128)(2,1)S(1)} %slice.55), channel_id=1, source_target_pairs={{0,12},{4,0},{8,4},{12,8},{1,13},{5,1},{9,5},{13,9},{2,14},{6,2},{... | collective-permute-start | bytes 1572872 | tf_op jit(solution)/shard_map/ppermute | solution.py:197
  57.1 8.1 %collective-permute-done.15 = bf16[2,256,512]{2,1,0:T(8,128)(2,1)S(1)} collective-permute-done((bf16[2,256,512]{2,1,0:T(8,128)(2,1)S(1)}, bf16[2,256,512]{2,1,0:T(8,128)(2,1)S(1)}, u32[]{:S(2)}, u32[]{:S(2)}) %collective-permute-start.15) | collective-permute-done | bytes 524320 | tf_op jit(solution)/shard_map/ppermute | solution.py:196
  66.8 1.1 constant_dynamic-update-slice_fusion
  67.9 2.1 collective-permute-start.17
  70.2 3.1 %collective-permute-start.19 = (bf16[256,1024]{1,0:T(8,128)(2,1)S(1)}, bf16[256,1024]{1,0:T(8,128)(2,1)S(1)}, u32[]{:S(2)}, u32[]{:S(2)}) collective-permute-start(bf16[256,1024]{1,0:T(8,128)(2,1)S(1)} %bitcast.29), channel_id=1, source_target_pairs={{0,64},{64,128},{128,192},{192,0},{1,65},{65,129},{129,193},{193,1... | collective-permute-start | bytes 1572872 | tf_op jit(solution)/shard_map/ppermute | solution.py:206
  73.2 3.3 %collective-permute-start.18 = (bf16[256,1024]{1,0:T(8,128)(2,1)S(1)}, bf16[256,1024]{1,0:T(8,128)(2,1)S(1)}, u32[]{:S(2)}, u32[]{:S(2)}) collective-permute-start(bf16[256,1024]{1,0:T(8,128)(2,1)S(1)} %bitcast.30), channel_id=1, source_target_pairs={{0,192},{64,0},{128,64},{192,128},{1,193},{65,1},{129,65},{193,129... | collective-permute-start | bytes 1572872 | tf_op jit(solution)/shard_map/ppermute | solution.py:207
  76.5 16.6 %collective-permute-done.19.prev = bf16[256,1024]{1,0:T(8,128)(2,1)S(1)} collective-permute-done((bf16[256,1024]{1,0:T(8,128)(2,1)S(1)}, bf16[256,1024]{1,0:T(8,128)(2,1)S(1)}, u32[]{:S(2)}, u32[]{:S(2)}) %collective-permute-start.19) | collective-permute-done | bytes 524320 | tf_op jit(solution)/shard_map/ppermute | solution.py:206
  93.2 7.0 %collective-permute-start.20 = (bf16[128,1024]{1,0:T(8,128)(2,1)S(1)}, bf16[128,1024]{1,0:T(8,128)(2,1)S(1)}, u32[]{:S(2)}, u32[]{:S(2)}) collective-permute-start(bf16[128,1024]{1,0:T(8,128)(2,1)S(1)} %slice.56), channel_id=1, source_target_pairs={{0,64},{64,128},{128,192},{192,0},{1,65},{65,129},{129,193},{193,1... | collective-permute-start | bytes 786440 | tf_op jit(solution)/shard_map/ppermute | solution.py:208
  100.2 1.2 collective-permute-start
  101.4 4.3 %collective-permute-start.4 = (bf16[256,1024]{1,0:T(8,128)(2,1)S(1)}, bf16[256,1024]{1,0:T(8,128)(2,1)S(1)}, u32[]{:S(2)}, u32[]{:S(2)}) collective-permute-start(bf16[256,1024]{1,0:T(8,128)(2,1)S(1)} %bitcast.25), channel_id=1, source_target_pairs={{0,64},{64,128},{128,192},{192,0},{1,65},{65,129},{129,193},{193,1... | collective-permute-start | bytes 1572872 | tf_op jit(solution)/shard_map/ppermute | solution.py:206
  107.3 8.9 %collective-permute-done.20.opp_a = bf16[128,1024]{1,0:T(8,128)(2,1)S(1)} collective-permute-done((bf16[128,1024]{1,0:T(8,128)(2,1)S(1)}, bf16[128,1024]{1,0:T(8,128)(2,1)S(1)}, u32[]{:S(2)}, u32[]{:S(2)}) %collective-permute-start.20) | collective-permute-done | bytes 262176 | tf_op jit(solution)/shard_map/ppermute | solution.py:208
  116.3 25.0 %collective-permute-done.21.opp_b = bf16[128,1024]{1,0:T(8,128)(2,1)} collective-permute-done((bf16[128,1024]{1,0:T(8,128)(2,1)}, bf16[128,1024]{1,0:T(8,128)(2,1)}, u32[]{:S(2)}, u32[]{:S(2)}) %collective-permute-start.21) | collective-permute-done | bytes 262176 | tf_op jit(solution)/shard_map/ppermute | solution.py:209
  141.4 6.7 %shard_map.87 = bf16[8,2,32,512]{3,2,1,0:T(8,128)(2,1)} custom-call(s32[4]{0:T(128)S(1)} %pad_add_fusion.where_ref, bf16[256,1024]{1,0:T(8,128)(2,1)S(1)} %bitcast.31, bf16[256,1024]{1,0:T(8,128)(2,1)S(1)} %collective-permute-done.18.nxt, bf16[128,1024]{1,0:T(8,128)(2,1)S(1)} %collective-permute-done.20.opp_a, ...), custom_call_target="tpu_custom_call" | custom-call | tf_op jit(solution)/shard_map/pallas_call | solution.py:43
  148.1 3.8 %all-to-all-start.1 = ((bf16[16,32,512]{2,1,0:T(8,128)(2,1)}), bf16[16,32,512]{2,1,0:T(8,128)(2,1)S(1)}, u32[]{:S(2)}, u32[]{:S(2)}) async-start(bf16[16,32,512]{2,1,0:T(8,128)(2,1)} %bitcast.19), calls=%async_computation.1 | async-start | bytes 1048576 | tf_op jit(solution)/shard_map/all_to_all | solution.py:226
  151.9 1.4 maximum_select_fusion.1
  154.4 3.1 %collective-permute-start.5 = (bf16[128,1024]{1,0:T(8,128)(2,1)S(1)}, bf16[128,1024]{1,0:T(8,128)(2,1)S(1)}, u32[]{:S(2)}, u32[]{:S(2)}) collective-permute-start(bf16[128,1024]{1,0:T(8,128)(2,1)S(1)} %slice.52), channel_id=1, source_target_pairs={{0,64},{64,128},{128,192},{192,0},{1,65},{65,129},{129,193},{193,1... | collective-permute-start | bytes 786440 | tf_op jit(solution)/shard_map/ppermute | solution.py:208
  158.1 8.6 %collective-permute-done.5.opp_a = bf16[128,1024]{1,0:T(8,128)(2,1)S(1)} collective-permute-done((bf16[128,1024]{1,0:T(8,128)(2,1)S(1)}, bf16[128,1024]{1,0:T(8,128)(2,1)S(1)}, u32[]{:S(2)}, u32[]{:S(2)}) %collective-permute-start.5) | collective-permute-done | bytes 262176 | tf_op jit(solution)/shard_map/ppermute | solution.py:208
  166.7 3.2 %collective-permute-done.6.opp_b = bf16[128,1024]{1,0:T(8,128)(2,1)S(1)} collective-permute-done((bf16[128,1024]{1,0:T(8,128)(2,1)S(1)}, bf16[128,1024]{1,0:T(8,128)(2,1)S(1)}, u32[]{:S(2)}, u32[]{:S(2)}) %collective-permute-start.6) | collective-permute-done | bytes 262176 | tf_op jit(solution)/shard_map/ppermute | solution.py:209
  169.9 6.6 %shard_map.86 = bf16[8,2,32,512]{3,2,1,0:T(8,128)(2,1)} custom-call(s32[4]{0:T(128)S(1)} %pad_add_fusion.where_ref, bf16[256,1024]{1,0:T(8,128)(2,1)S(1)} %bitcast.27, bf16[256,1024]{1,0:T(8,128)(2,1)S(1)} %collective-permute-done.3.nxt, bf16[128,1024]{1,0:T(8,128)(2,1)S(1)} %collective-permute-done.5.opp_a, ...), custom_call_target="tpu_custom_call" | custom-call | tf_op jit(solution)/shard_map/pallas_call | solution.py:43
  176.6 7.9 %all-to-all-start = ((bf16[16,32,512]{2,1,0:T(8,128)(2,1)}), bf16[16,32,512]{2,1,0:T(8,128)(2,1)}, u32[]{:S(2)}, u32[]{:S(2)}) async-start(bf16[16,32,512]{2,1,0:T(8,128)(2,1)} %bitcast.16), calls=%async_computation | async-start | bytes 1048576 | tf_op jit(solution)/shard_map/all_to_all | solution.py:226
  185.8 1.4 maximum_select_fusion.q_ref
  188.3 2.7 %shard_map.88 = (f32[8,256,256]{2,1,0:T(8,128)S(1)}, f32[8,8,256]{2,1,0:T(8,128)S(1)}) custom-call(s32[6]{0:T(128)S(1)} %stack.57.where_ref, bf16[2048,256]{1,0:T(8,128)(2,1)S(1)} %maximum_select_fusion.q_ref, bf16[512,512]{1,0:T(8,128)(2,1)S(1)} %bitcast.28), custom_call_target="tpu_custom_call" | custom-call | tf_op jit(solution)/shard_map/pallas_call | solution.py:43
  191.0 4.7 %all-to-all-done = bf16[16,32,512]{2,1,0:T(8,128)(2,1)} async-done(((bf16[16,32,512]{2,1,0:T(8,128)(2,1)}), bf16[16,32,512]{2,1,0:T(8,128)(2,1)}, u32[]{:S(2)}, u32[]{:S(2)}) %all-to-all-start) | async-done | bytes 524320 | tf_op jit(solution)/shard_map/all_to_all | solution.py:226
  195.8 3.5 %shard_map.89 = (bf16[2,272,256]{2,1,0:T(8,128)(2,1)S(1)}, bf16[2,272,256]{2,1,0:T(8,128)(2,1)S(1)}, bf16[2,272,256]{2,1,0:T(8,128)(2,1)S(1)}, bf16[2,272,256]{2,1,0:T(8,128)(2,1)S(1)}) custom-call(s32[6]{0:T(128)S(1)} %stack.57.where_ref, bf16[2048,256]{1,0:T(8,128)(2,1)S(1)} %maximum_select_fusion.q_ref, bf16[512,512]{1,0:T(8,128)(2,1)} %bitcast.17.kv_ref, ...), custom_call_target="tpu_custom_call" | custom-call | tf_op jit(solution)/shard_map/pallas_call | solution.py:43
  199.3 1.9 collective-permute-start.22
  201.2 1.3 collective-permute-start.24
  202.5 4.4 %collective-permute-done.22.b_ref = bf16[2,272,256]{2,1,0:T(8,128)(2,1)S(1)} collective-permute-done((bf16[2,272,256]{2,1,0:T(8,128)(2,1)S(1)}, bf16[2,272,256]{2,1,0:T(8,128)(2,1)S(1)}, u32[]{:S(2)}, u32[]{:S(2)}) %collective-permute-start.22) | collective-permute-done | bytes 278560 | tf_op jit(solution)/shard_map/ppermute | solution.py:25
  206.9 7.0 %collective-permute-done.23.c_ref = bf16[2,272,256]{2,1,0:T(8,128)(2,1)S(1)} collective-permute-done((bf16[2,272,256]{2,1,0:T(8,128)(2,1)S(1)}, bf16[2,272,256]{2,1,0:T(8,128)(2,1)S(1)}, u32[]{:S(2)}, u32[]{:S(2)}) %collective-permute-start.23) | collective-permute-done | bytes 278560 | tf_op jit(solution)/shard_map/ppermute | solution.py:25
  214.7 2.5 collective-permute-start.25
  218.2 1.8 shard_map.91
  220.0 1.1 collective-permute-start.30
  221.1 1.3 collective-permute-start.26
  222.4 2.4 collective-permute-start.28
  224.9 1.1 collective-permute-start.29
  226.0 20.0 %collective-permute-done.30 = bf16[32,4096]{1,0:T(8,128)(2,1)S(1)} collective-permute-done((bf16[32,4096]{1,0:T(8,128)(2,1)S(1)}, bf16[32,4096]{1,0:T(8,128)(2,1)S(1)}, u32[]{:S(2)}, u32[]{:S(2)}) %collective-permute-start.30) | collective-permute-done | bytes 262176 | tf_op jit(solution)/shard_map/ppermute | solution.py:240
  246.2 2.4 collective-permute-start.27
  248.6 3.0 %collective-permute-done.29.next_a = bf16[32,4096]{1,0:T(8,128)(2,1)S(1)} collective-permute-done((bf16[32,4096]{1,0:T(8,128)(2,1)S(1)}, bf16[32,4096]{1,0:T(8,128)(2,1)S(1)}, u32[]{:S(2)}, u32[]{:S(2)}) %collective-permute-start.29) | collective-permute-done | bytes 262176 | tf_op jit(solution)/shard_map/ppermute | solution.py:242
  251.7 5.6 %collective-permute-done.31.next_b = bf16[32,4096]{1,0:T(8,128)(2,1)S(1)} collective-permute-done((bf16[32,4096]{1,0:T(8,128)(2,1)S(1)}, bf16[32,4096]{1,0:T(8,128)(2,1)S(1)}, u32[]{:S(2)}, u32[]{:S(2)}) %collective-permute-start.31) | collective-permute-done | bytes 262176 | tf_op jit(solution)/shard_map/ppermute | solution.py:246
  257.6 1.9 shard_map.92
  (72 shorter events, 17.1 us)
Async XLA Ops:
  1.5 4.7 %collective-permute-start.7 = (bf16[64,512]{1,0:T(8,128)(2,1)S(1)}, bf16[64,512]{1,0:T(8,128)(2,1)S(1)}, u32[]{:S(2)}, u32[]{:S(2)}) collective-permute-start(bf16[64,512]{1,0:T(8,128)(2,1)S(1)} %get-tuple-element.39), channel_id=1, source_target_pairs={{0,1},{1,0},{2,3},{3,2},{4,5},{5,4},{6,7},{7,6},{8,9},{9,8},{10,11... | collective-permute-start | bytes 196616 | tf_op jit(solution)/shard_map/ppermute | solution.py:25
  4.8 4.9 %collective-permute-start.9 = (bf16[64,512]{1,0:T(8,128)(2,1)S(1)}, bf16[64,512]{1,0:T(8,128)(2,1)S(1)}, u32[]{:S(2)}, u32[]{:S(2)}) collective-permute-start(bf16[64,512]{1,0:T(8,128)(2,1)S(1)} %get-tuple-element.39), channel_id=1, source_target_pairs={{0,3},{1,2},{2,1},{3,0},{4,7},{5,6},{6,5},{7,4},{8,11},{9,10},{10,... | collective-permute-start | bytes 196616 | tf_op jit(solution)/shard_map/ppermute | solution.py:190
  4.8 4.9 %collective-permute-start.8 = (bf16[64,512]{1,0:T(8,128)(2,1)S(1)}, bf16[64,512]{1,0:T(8,128)(2,1)S(1)}, u32[]{:S(2)}, u32[]{:S(2)}) collective-permute-start(bf16[64,512]{1,0:T(8,128)(2,1)S(1)} %get-tuple-element.38), channel_id=1, source_target_pairs={{0,2},{2,0},{1,3},{3,1},{4,6},{6,4},{5,7},{7,5},{8,10},{10,8},{9,1... | collective-permute-start | bytes 196616 | tf_op jit(solution)/shard_map/ppermute | solution.py:25
  9.8 7.0 %collective-permute-start.10 = (bf16[256,512]{1,0:T(8,128)(2,1)S(1)}, bf16[256,512]{1,0:T(8,128)(2,1)S(1)}, u32[]{:S(2)}, u32[]{:S(2)}) collective-permute-start(bf16[256,512]{1,0:T(8,128)(2,1)S(1)} %maximum_select_fusion.4), channel_id=1, source_target_pairs={{0,48},{16,0},{32,16},{48,32},{1,49},{17,1},{33,17},{49,33},{2,50}... | collective-permute-start | bytes 786440 | tf_op jit(solution)/shard_map/ppermute | solution.py:29
  10.5 7.6 %collective-permute-start.11 = (bf16[256,512]{1,0:T(8,128)(2,1)S(1)}, bf16[256,512]{1,0:T(8,128)(2,1)S(1)}, u32[]{:S(2)}, u32[]{:S(2)}) collective-permute-start(bf16[256,512]{1,0:T(8,128)(2,1)S(1)} %maximum_select_fusion.4), channel_id=1, source_target_pairs={{0,32},{16,48},{32,0},{48,16},{1,33},{17,49},{33,1},{49,17},{2,34}... | collective-permute-start | bytes 786440 | tf_op jit(solution)/shard_map/ppermute | solution.py:29
  11.0 14.8 %collective-permute-start.12 = (bf16[256,512]{1,0:T(8,128)(2,1)S(1)}, bf16[256,512]{1,0:T(8,128)(2,1)S(1)}, u32[]{:S(2)}, u32[]{:S(2)}) collective-permute-start(bf16[256,512]{1,0:T(8,128)(2,1)S(1)} %maximum_select_fusion.4), channel_id=1, source_target_pairs={{0,16},{16,32},{32,48},{48,0},{1,17},{17,33},{33,49},{49,1},{2,18}... | collective-permute-start | bytes 786440 | tf_op jit(solution)/shard_map/ppermute | solution.py:29
  26.0 25.6 %collective-permute-start.14 = (bf16[4,256,512]{2,1,0:T(8,128)(2,1)S(1)}, bf16[4,256,512]{2,1,0:T(8,128)(2,1)S(1)}, u32[]{:S(2)}, u32[]{:S(2)}) collective-permute-start(bf16[4,256,512]{2,1,0:T(8,128)(2,1)S(1)} %pad_maximum_fusion), channel_id=1, source_target_pairs={{0,4},{4,8},{8,12},{12,0},{1,5},{5,9},{9,13},{13,1},{2,6},{6,10},{... | collective-permute-start | bytes 3145736 | tf_op jit(solution)/shard_map/ppermute | solution.py:194
  27.4 24.4 %collective-permute-start.13 = (bf16[4,256,512]{2,1,0:T(8,128)(2,1)S(1)}, bf16[4,256,512]{2,1,0:T(8,128)(2,1)S(1)}, u32[]{:S(2)}, u32[]{:S(2)}) collective-permute-start(bf16[4,256,512]{2,1,0:T(8,128)(2,1)S(1)} %pad_maximum_fusion), channel_id=1, source_target_pairs={{0,12},{4,0},{8,4},{12,8},{1,13},{5,1},{9,5},{13,9},{2,14},{6,2},{... | collective-permute-start | bytes 3145736 | tf_op jit(solution)/shard_map/ppermute | solution.py:195
  51.7 18.4 %copy-start.5 = (bf16[8,64,1024]{2,1,0:T(8,128)(2,1)S(1)}, bf16[8,64,1024]{2,1,0:T(8,128)(2,1)}, u32[]{:S(2)}) copy-start(bf16[8,64,1024]{2,1,0:T(8,128)(2,1)} %param.7) | copy-start | bytes 3145732
  51.7 13.5 %collective-permute-start.15 = (bf16[2,256,512]{2,1,0:T(8,128)(2,1)S(1)}, bf16[2,256,512]{2,1,0:T(8,128)(2,1)S(1)}, u32[]{:S(2)}, u32[]{:S(2)}) collective-permute-start(bf16[2,256,512]{2,1,0:T(8,128)(2,1)S(1)} %slice.54), channel_id=1, source_target_pairs={{0,4},{4,8},{8,12},{12,0},{1,5},{5,9},{9,13},{13,1},{2,6},{6,10},{... | collective-permute-start | bytes 1572872 | tf_op jit(solution)/shard_map/ppermute | solution.py:196
  51.8 14.2 %collective-permute-start.16 = (bf16[2,256,512]{2,1,0:T(8,128)(2,1)S(1)}, bf16[2,256,512]{2,1,0:T(8,128)(2,1)S(1)}, u32[]{:S(2)}, u32[]{:S(2)}) collective-permute-start(bf16[2,256,512]{2,1,0:T(8,128)(2,1)S(1)} %slice.55), channel_id=1, source_target_pairs={{0,12},{4,0},{8,4},{12,8},{1,13},{5,1},{9,5},{13,9},{2,14},{6,2},{... | collective-permute-start | bytes 1572872 | tf_op jit(solution)/shard_map/ppermute | solution.py:197
  56.0 44.1 %copy-start.6 = (bf16[256,512]{1,0:T(8,128)(2,1)S(1)}, bf16[256,512]{1,0:T(8,128)(2,1)}, u32[]{:S(2)}) copy-start(bf16[256,512]{1,0:T(8,128)(2,1)} %param.10) | copy-start | bytes 786436
  67.9 73.5 %collective-permute-start.17 = (bf16[4,4,256,512]{3,2,1,0:T(8,128)(2,1)}, bf16[4,4,256,512]{3,2,1,0:T(8,128)(2,1)}, u32[]{:S(2)}, u32[]{:S(2)}) collective-permute-start(bf16[4,4,256,512]{3,2,1,0:T(8,128)(2,1)} %bitcast.15.w_mine), channel_id=1, source_target_pairs={{0,1},{1,0},{2,3},{3,2},{4,5},{5,4},{6,7},{7,6},{8,9},{9,8},{10,11... | collective-permute-start | bytes 12582920 | tf_op jit(solution)/shard_map/ppermute | solution.py:25
  70.2 23.0 %collective-permute-start.19 = (bf16[256,1024]{1,0:T(8,128)(2,1)S(1)}, bf16[256,1024]{1,0:T(8,128)(2,1)S(1)}, u32[]{:S(2)}, u32[]{:S(2)}) collective-permute-start(bf16[256,1024]{1,0:T(8,128)(2,1)S(1)} %bitcast.29), channel_id=1, source_target_pairs={{0,64},{64,128},{128,192},{192,0},{1,65},{65,129},{129,193},{193,1... | collective-permute-start | bytes 1572872 | tf_op jit(solution)/shard_map/ppermute | solution.py:206
  73.2 32.5 %collective-permute-start.18 = (bf16[256,1024]{1,0:T(8,128)(2,1)S(1)}, bf16[256,1024]{1,0:T(8,128)(2,1)S(1)}, u32[]{:S(2)}, u32[]{:S(2)}) collective-permute-start(bf16[256,1024]{1,0:T(8,128)(2,1)S(1)} %bitcast.30), channel_id=1, source_target_pairs={{0,192},{64,0},{128,64},{192,128},{1,193},{65,1},{129,65},{193,129... | collective-permute-start | bytes 1572872 | tf_op jit(solution)/shard_map/ppermute | solution.py:207
  93.2 23.1 %collective-permute-start.20 = (bf16[128,1024]{1,0:T(8,128)(2,1)S(1)}, bf16[128,1024]{1,0:T(8,128)(2,1)S(1)}, u32[]{:S(2)}, u32[]{:S(2)}) collective-permute-start(bf16[128,1024]{1,0:T(8,128)(2,1)S(1)} %slice.56), channel_id=1, source_target_pairs={{0,64},{64,128},{128,192},{192,0},{1,65},{65,129},{129,193},{193,1... | collective-permute-start | bytes 786440 | tf_op jit(solution)/shard_map/ppermute | solution.py:208
  100.2 6.2 %collective-permute-start = (bf16[256,256]{1,0:T(8,128)(2,1)S(1)}, bf16[256,256]{1,0:T(8,128)(2,1)S(1)}, u32[]{:S(2)}, u32[]{:S(2)}) collective-permute-start(bf16[256,256]{1,0:T(8,128)(2,1)S(1)} %get-tuple-element.37), channel_id=1, source_target_pairs={{0,1},{1,0},{2,3},{3,2},{4,5},{5,4},{6,7},{7,6},{8,9},{9,8},{10,11... | collective-permute-start | bytes 393224 | tf_op jit(solution)/shard_map/ppermute | solution.py:25
  101.4 53.0 %collective-permute-start.4 = (bf16[256,1024]{1,0:T(8,128)(2,1)S(1)}, bf16[256,1024]{1,0:T(8,128)(2,1)S(1)}, u32[]{:S(2)}, u32[]{:S(2)}) collective-permute-start(bf16[256,1024]{1,0:T(8,128)(2,1)S(1)} %bitcast.25), channel_id=1, source_target_pairs={{0,64},{64,128},{128,192},{192,0},{1,65},{65,129},{129,193},{193,1... | collective-permute-start | bytes 1572872 | tf_op jit(solution)/shard_map/ppermute | solution.py:206
  105.7 51.8 %collective-permute-start.3 = (bf16[256,1024]{1,0:T(8,128)(2,1)S(1)}, bf16[256,1024]{1,0:T(8,128)(2,1)S(1)}, u32[]{:S(2)}, u32[]{:S(2)}) collective-permute-start(bf16[256,1024]{1,0:T(8,128)(2,1)S(1)} %bitcast.26), channel_id=1, source_target_pairs={{0,192},{64,0},{128,64},{192,128},{1,193},{65,1},{129,65},{193,129... | collective-permute-start | bytes 1572872 | tf_op jit(solution)/shard_map/ppermute | solution.py:207
  106.4 35.0 %collective-permute-start.21 = (bf16[128,1024]{1,0:T(8,128)(2,1)}, bf16[128,1024]{1,0:T(8,128)(2,1)}, u32[]{:S(2)}, u32[]{:S(2)}) collective-permute-start(bf16[128,1024]{1,0:T(8,128)(2,1)} %slice.57), channel_id=1, source_target_pairs={{0,192},{64,0},{128,64},{192,128},{1,193},{65,1},{129,65},{193,129... | collective-permute-start | bytes 786440 | tf_op jit(solution)/shard_map/ppermute | solution.py:209
  116.3 35.6 %collective-permute-start.1 = (bf16[512,256]{1,0:T(8,128)(2,1)}, bf16[512,256]{1,0:T(8,128)(2,1)}, u32[]{:S(2)}, u32[]{:S(2)}) collective-permute-start(bf16[512,256]{1,0:T(8,128)(2,1)} %maximum_select_fusion.2), channel_id=1, source_target_pairs={{0,2},{2,0},{1,3},{3,1},{4,6},{6,4},{5,7},{7,5},{8,10},{10,8},{9,1... | collective-permute-start | bytes 786440 | tf_op jit(solution)/shard_map/ppermute | solution.py:25
  148.1 28.5 %all-to-all-start.1 = ((bf16[16,32,512]{2,1,0:T(8,128)(2,1)}), bf16[16,32,512]{2,1,0:T(8,128)(2,1)S(1)}, u32[]{:S(2)}, u32[]{:S(2)}) async-start(bf16[16,32,512]{2,1,0:T(8,128)(2,1)} %bitcast.19), calls=%async_computation.1 | async-start | bytes 1048576 | tf_op jit(solution)/shard_map/all_to_all | solution.py:226
  153.3 32.5 %collective-permute-start.2 = (bf16[1024,256]{1,0:T(8,128)(2,1)S(1)}, bf16[1024,256]{1,0:T(8,128)(2,1)}, u32[]{:S(2)}, u32[]{:S(2)}) collective-permute-start(bf16[1024,256]{1,0:T(8,128)(2,1)S(1)} %maximum_select_fusion.1), channel_id=1, source_target_pairs={{0,4},{4,0},{1,5},{5,1},{2,6},{6,2},{3,7},{7,3},{8,12},{12,8},{9,1... | collective-permute-start | bytes 1572872 | tf_op jit(solution)/shard_map/ppermute | solution.py:25
  154.4 12.4 %collective-permute-start.5 = (bf16[128,1024]{1,0:T(8,128)(2,1)S(1)}, bf16[128,1024]{1,0:T(8,128)(2,1)S(1)}, u32[]{:S(2)}, u32[]{:S(2)}) collective-permute-start(bf16[128,1024]{1,0:T(8,128)(2,1)S(1)} %slice.52), channel_id=1, source_target_pairs={{0,64},{64,128},{128,192},{192,0},{1,65},{65,129},{129,193},{193,1... | collective-permute-start | bytes 786440 | tf_op jit(solution)/shard_map/ppermute | solution.py:208
  157.5 27.0 %copy-start.7 = (s32[8]{0:T(128)S(1)}, s32[8]{0:T(128)}, u32[]{:S(2)}) copy-start(s32[8]{0:T(128)} %param.9) | copy-start | bytes 100
  157.5 12.4 %collective-permute-start.6 = (bf16[128,1024]{1,0:T(8,128)(2,1)S(1)}, bf16[128,1024]{1,0:T(8,128)(2,1)S(1)}, u32[]{:S(2)}, u32[]{:S(2)}) collective-permute-start(bf16[128,1024]{1,0:T(8,128)(2,1)S(1)} %slice.53), channel_id=1, source_target_pairs={{0,192},{64,0},{128,64},{192,128},{1,193},{65,1},{129,65},{193,129... | collective-permute-start | bytes 786440 | tf_op jit(solution)/shard_map/ppermute | solution.py:209
  176.6 10.7 %copy-start.1 = (bf16[16,32,512]{2,1,0:T(8,128)(2,1)}, bf16[16,32,512]{2,1,0:T(8,128)(2,1)S(1)}, u32[]{:S(2)}) copy-start(bf16[16,32,512]{2,1,0:T(8,128)(2,1)S(1)} %all-to-all-done.1) | copy-start | bytes 1572868
  176.6 19.2 %all-to-all-start = ((bf16[16,32,512]{2,1,0:T(8,128)(2,1)}), bf16[16,32,512]{2,1,0:T(8,128)(2,1)}, u32[]{:S(2)}, u32[]{:S(2)}) async-start(bf16[16,32,512]{2,1,0:T(8,128)(2,1)} %bitcast.16), calls=%async_computation | async-start | bytes 1048576 | tf_op jit(solution)/shard_map/all_to_all | solution.py:226
  187.3 1.0 copy-start.2
  195.8 22.4 %copy-start = (bf16[512,4096]{1,0:T(8,128)(2,1)S(1)}, bf16[512,4096]{1,0:T(8,128)(2,1)}, u32[]{:S(2)}) copy-start(bf16[512,4096]{1,0:T(8,128)(2,1)} %w_ref.1) | copy-start | bytes 12582916
  199.3 58.4 %copy-start.3 = (bf16[64,4096]{1,0:T(8,128)(2,1)S(1)}, bf16[64,4096]{1,0:T(8,128)(2,1)}, u32[]{:S(2)}) copy-start(bf16[64,4096]{1,0:T(8,128)(2,1)} %residual.1) | copy-start | bytes 1572868
  199.3 58.4 %copy-start.4 = (f32[4096]{0:T(1024)S(1)}, f32[4096]{0:T(1024)}, u32[]{:S(2)}) copy-start(f32[4096]{0:T(1024)} %param.13) | copy-start | bytes 49156
  199.3 7.6 %collective-permute-start.22 = (bf16[2,272,256]{2,1,0:T(8,128)(2,1)S(1)}, bf16[2,272,256]{2,1,0:T(8,128)(2,1)S(1)}, u32[]{:S(2)}, u32[]{:S(2)}) collective-permute-start(bf16[2,272,256]{2,1,0:T(8,128)(2,1)S(1)} %get-tuple-element.20), channel_id=1, source_target_pairs={{0,2},{2,0},{1,3},{3,1},{4,6},{6,4},{5,7},{7,5},{8,10},{10,8},{9,1... | collective-permute-start | bytes 835592 | tf_op jit(solution)/shard_map/ppermute | solution.py:25
  201.2 12.7 %collective-permute-start.23 = (bf16[2,272,256]{2,1,0:T(8,128)(2,1)S(1)}, bf16[2,272,256]{2,1,0:T(8,128)(2,1)S(1)}, u32[]{:S(2)}, u32[]{:S(2)}) collective-permute-start(bf16[2,272,256]{2,1,0:T(8,128)(2,1)S(1)} %get-tuple-element.21), channel_id=1, source_target_pairs={{0,4},{4,0},{1,5},{5,1},{2,6},{6,2},{3,7},{7,3},{8,12},{12,8},{9,1... | collective-permute-start | bytes 835592 | tf_op jit(solution)/shard_map/ppermute | solution.py:25
  201.2 12.7 %collective-permute-start.24 = (bf16[2,272,256]{2,1,0:T(8,128)(2,1)S(1)}, bf16[2,272,256]{2,1,0:T(8,128)(2,1)S(1)}, u32[]{:S(2)}, u32[]{:S(2)}) collective-permute-start(bf16[2,272,256]{2,1,0:T(8,128)(2,1)S(1)} %get-tuple-element.22), channel_id=1, source_target_pairs={{0,6},{2,4},{4,2},{6,0},{1,7},{3,5},{5,3},{7,1},{8,14},{10,12},{12... | collective-permute-start | bytes 835592 | tf_op jit(solution)/shard_map/ppermute | solution.py:234
  214.7 3.4 %collective-permute-start.25 = (bf16[256,256]{1,0:T(8,128)(2,1)S(1)}, bf16[256,256]{1,0:T(8,128)(2,1)S(1)}, u32[]{:S(2)}, u32[]{:S(2)}) collective-permute-start(bf16[256,256]{1,0:T(8,128)(2,1)S(1)} %get-tuple-element.24), channel_id=1, source_target_pairs={{0,1},{1,0},{2,3},{3,2},{4,5},{5,4},{6,7},{7,6},{8,9},{9,8},{10,11... | collective-permute-start | bytes 393224 | tf_op jit(solution)/shard_map/ppermute | solution.py:25
  220.0 26.0 %collective-permute-start.30 = (bf16[32,4096]{1,0:T(8,128)(2,1)S(1)}, bf16[32,4096]{1,0:T(8,128)(2,1)S(1)}, u32[]{:S(2)}, u32[]{:S(2)}) collective-permute-start(bf16[32,4096]{1,0:T(8,128)(2,1)S(1)} %get-tuple-element.31), channel_id=1, source_target_pairs={{0,192},{64,0},{128,64},{192,128},{1,193},{65,1},{129,65},{193,129... | collective-permute-start | bytes 786440 | tf_op jit(solution)/shard_map/ppermute | solution.py:240
  221.1 25.1 %collective-permute-start.26 = (bf16[32,4096]{1,0:T(8,128)(2,1)S(1)}, bf16[32,4096]{1,0:T(8,128)(2,1)S(1)}, u32[]{:S(2)}, u32[]{:S(2)}) collective-permute-start(bf16[32,4096]{1,0:T(8,128)(2,1)S(1)} %get-tuple-element.27), channel_id=1, source_target_pairs={{0,64},{64,128},{128,192},{192,0},{1,65},{65,129},{129,193},{193,1... | collective-permute-start | bytes 786440 | tf_op jit(solution)/shard_map/ppermute | solution.py:239
  222.4 26.2 %collective-permute-start.28 = (bf16[32,4096]{1,0:T(8,128)(2,1)S(1)}, bf16[32,4096]{1,0:T(8,128)(2,1)S(1)}, u32[]{:S(2)}, u32[]{:S(2)}) collective-permute-start(bf16[32,4096]{1,0:T(8,128)(2,1)S(1)} %get-tuple-element.28), channel_id=1, source_target_pairs={{0,64},{64,128},{128,192},{192,0},{1,65},{65,129},{129,193},{193,1... | collective-permute-start | bytes 786440 | tf_op jit(solution)/shard_map/ppermute | solution.py:241
  224.9 26.8 %collective-permute-start.29 = (bf16[32,4096]{1,0:T(8,128)(2,1)S(1)}, bf16[32,4096]{1,0:T(8,128)(2,1)S(1)}, u32[]{:S(2)}, u32[]{:S(2)}) collective-permute-start(bf16[32,4096]{1,0:T(8,128)(2,1)S(1)} %get-tuple-element.29), channel_id=1, source_target_pairs={{0,192},{64,0},{128,64},{192,128},{1,193},{65,1},{129,65},{193,129... | collective-permute-start | bytes 786440 | tf_op jit(solution)/shard_map/ppermute | solution.py:242
  246.1 11.2 %collective-permute-start.31 = (bf16[32,4096]{1,0:T(8,128)(2,1)S(1)}, bf16[32,4096]{1,0:T(8,128)(2,1)S(1)}, u32[]{:S(2)}, u32[]{:S(2)}) collective-permute-start(bf16[32,4096]{1,0:T(8,128)(2,1)S(1)} %add_convert_fusion), channel_id=1, source_target_pairs={{0,192},{64,0},{128,64},{192,128},{1,193},{65,1},{129,65},{193,129... | collective-permute-start | bytes 786440 | tf_op jit(solution)/shard_map/ppermute | solution.py:246
  246.2 11.4 %collective-permute-start.27 = (bf16[32,4096]{1,0:T(8,128)(2,1)S(1)}, bf16[32,4096]{1,0:T(8,128)(2,1)S(1)}, u32[]{:S(2)}, u32[]{:S(2)}) collective-permute-start(bf16[32,4096]{1,0:T(8,128)(2,1)S(1)} %add_convert_fusion.1), channel_id=1, source_target_pairs={{0,64},{64,128},{128,192},{192,0},{1,65},{65,129},{129,193},{193,1... | collective-permute-start | bytes 786440 | tf_op jit(solution)/shard_map/ppermute | solution.py:245
